TPU v7x, 256 devices: a whole 4x4x8 slice. The times are simulated.
256 devices in a mesh: lat: 4 (over y), lon: 64 (over z, x, core).
Axes of the slice: x: 4, y: 4, z: 8, core: 2. Of those that a mesh axis runs over, the one named last changes fastest.
Arguments:
- model_state: float32 [5, 4, 3584, 1024], P(None, None, 'lon', 'lat'), may hold values from -6 to 6
- diffusion: float32 [2, 1024], P(None, 'lat'), may hold values from 0.02 to 0.24
- coupling: float32 [4, 5, 5], replicated, may hold values from -2.5 to 2.5
- cutoff: int32 [256], replicated, may hold values from 1 to 896, as said below
- strip_list: int32 [16384, 4], P(('lat', 'lon')), may hold values from 0 to 240, as said below
- nest_place: int32 [256, 64, 2], P(('lat', 'lon')), may hold values from 0 to 1872
Outputs:
- advanced_state: float32 [5, 4, 3584, 1024], P(None, None, 'lon', 'lat')
- nest_boundary: float32 [256, 5, 4, 2048], P(('lat', 'lon'))
Inputs may be any that keep to these rules, and one draw needn't show every extreme that they name: cutoff[b] is the number of kept wavenumbers of band row b; the values 1 and 896 both occur. `strip_list`: in the 64 rows of one device: column 0 names an owner (an index of lon) and no owner is named by more than 2 of these rows; at every index of lat some owner is named by exactly 2 rows of every device of that index. Column 1 is a longitude column within the device's block (below 56), column 2 a row offset within the block (at most 240), column 3 a length of 1 to 16; every device has a strip of length 16.
All inputs are finite; a program needn't handle non-finite values.
Results may differ from a plain program's by a relative error of at most 0.0001.
Values sent between devices are 32-bit elements; how exact they have to be, the bound alone decides.
A program may use at most 128 MiB of HBM per device.

v0:
```python
import math

import jax
import jax.numpy as jnp
from jax import lax
from jax.sharding import PartitionSpec as P

POLAR = 128
CAP = 2
STRIP = 16
RATIO = 11
NB = 2048
KC = 896


def padded_2(block, sides, width):
    for axis, dim in sides:
        count = lax.axis_size(axis)
        forward = [(i, i + 1) for i in range(count - 1)]
        forward.append((count - 1, 0))
        backward = [(target, source) for source, target in forward]
        low = lax.ppermute(
            lax.slice_in_dim(block, block.shape[dim] - width, None, axis=dim), axis, forward
        )
        high = lax.ppermute(lax.slice_in_dim(block, 0, width, axis=dim), axis, backward)
        block = jnp.concatenate([low, block, high], axis=dim)
    return block


def spectral_filter(rows, kept):
    top_wavenumber_kept = lax.Precision.HIGHEST
    length = rows.shape[3]
    width = math.gcd(KC, 128)
    column_grid = lax.broadcasted_iota(jnp.int32, (length, width), 0)
    step_output = jnp.zeros_like(rows)
    for block_index in range(KC // width):
        wavenumber = block_index * width + lax.broadcasted_iota(jnp.int32, (length, width), 1)
        phase = column_grid * wavenumber % length
        angle = phase.astype(jnp.float32) * (2.0 * math.pi / length)
        cosine = jnp.cos(angle)
        sine = jnp.sin(angle)
        along = block_index * width + jnp.arange(width, dtype=jnp.int32)
        scale = jnp.where(along == 0, 1.0 / length, 2.0 / length)
        weight = jnp.where(along[None, :] < kept[:, None], scale[None, :], 0.0)
        real_part = (
            jnp.einsum("flrn,nk->flrk", rows, cosine, precision=top_wavenumber_kept) * weight
        )
        imaginary_component = (
            jnp.einsum("flrn,nk->flrk", rows, sine, precision=top_wavenumber_kept) * weight
        )
        step_output = (
            step_output
            + jnp.einsum("flrk,nk->flrn", real_part, cosine, precision=top_wavenumber_kept)
            + jnp.einsum("flrk,nk->flrn", imaginary_component, sine, precision=top_wavenumber_kept)
        )
    return step_output


def polar_pass(work_rows, kept_start, kept_table):
    count = work_rows.shape[2] // lax.axis_size("lon")
    kept = lax.dynamic_slice_in_dim(kept_table, kept_start + lax.axis_index("lon") * count, count)
    return lax.all_to_all(
        spectral_filter(
            lax.all_to_all(work_rows, "lon", split_axis=2, concat_axis=3, tiled=True), kept
        ),
        "lon",
        split_axis=3,
        concat_axis=2,
        tiled=True,
    )


def local(model_state, diffusion, coupling, cutoff, strip_list, nest_place):
    top_wavenumber_kept = lax.Precision.HIGHEST
    lat_index = lax.axis_index("lat")
    lat_count = lax.axis_size("lat")
    lon_count = lax.axis_size("lon")
    fields, levels, lon_local, lat_local = model_state.shape
    padded = padded_2(model_state, (("lat", 3), ("lon", 2)), 1)
    east_west = padded[:, :, 2:, 1:-1] + padded[:, :, :-2, 1:-1]
    row_place = lax.broadcasted_iota(jnp.int32, (1, 1, 1, lat_local), 3)
    northern = jnp.where((lat_index == 0) & (row_place == 0), 0.0, padded[:, :, 1:-1, :-2])
    southern = jnp.where(
        (lat_index == lat_count - 1) & (row_place == lat_local - 1), 0.0, padded[:, :, 1:-1, 2:]
    )
    blended = jnp.einsum("lfg,glij->flij", coupling, model_state, precision=top_wavenumber_kept)
    updated = (
        model_state
        + diffusion[0] * (east_west - 2.0 * model_state)
        + diffusion[1] * (northern + southern - 2.0 * model_state)
        + blended
    )
    is_south = lat_index == lat_count - 1
    is_polar = (lat_index == 0) | is_south
    start = jnp.where(is_south, lat_local - POLAR, 0).astype(jnp.int32)
    band_base = jnp.where(lat_index < lat_count // 2, 0, POLAR).astype(jnp.int32)
    block_rows = lax.dynamic_slice_in_dim(updated, start, POLAR, 3)
    polar_rows = jnp.transpose(block_rows, (0, 1, 3, 2))
    filtered = polar_pass(polar_rows, band_base, cutoff)
    new_rows = jnp.where(is_polar, jnp.transpose(filtered, (0, 1, 3, 2)), block_rows)
    advanced_state = lax.dynamic_update_slice_in_dim(updated, new_rows, start, 3)
    slots = strip_list.shape[0]
    owners = strip_list[:, 0]
    columns = strip_list[:, 1]
    offsets = strip_list[:, 2]
    lengths = strip_list[:, 3]
    zero = jnp.zeros((), jnp.int32)

    def cut_strip(column, offset):
        return lax.dynamic_slice(
            updated, (zero, zero, column, offset), (fields, levels, 1, STRIP)
        ).reshape(fields * levels, STRIP)

    boundary_strips = jax.vmap(cut_strip)(columns, offsets)
    inside = lax.broadcasted_iota(jnp.int32, (1, 1, STRIP), 2) < lengths[:, None, None]
    boundary_strips = jnp.where(inside, boundary_strips, 0.0).reshape(
        slots, fields * levels * STRIP
    )
    slot_ids = jnp.arange(slots, dtype=jnp.int32)
    earlier = slot_ids[None, :] < slot_ids[:, None]
    same = owners[:, None] == owners[None, :]
    rank = jnp.sum((same & earlier).astype(jnp.int32), axis=1)
    target = owners * CAP + rank
    routing = (jnp.arange(lon_count * CAP, dtype=jnp.int32)[:, None] == target[None, :]).astype(
        jnp.float32
    )
    outgoing = jnp.dot(
        routing, boundary_strips, precision=top_wavenumber_kept, preferred_element_type=jnp.float32
    ).reshape(lon_count, CAP, fields * levels * STRIP)
    arrived = lax.all_to_all(outgoing, "lon", split_axis=0, concat_axis=0, tiled=True)
    total = lon_count * CAP
    group = math.gcd(total, 16)
    pieces = arrived.reshape(total // group, group, fields * levels, STRIP)
    starts = nest_place.reshape(total // group, group)
    point = lax.broadcasted_iota(jnp.int32, (1, 1, NB), 2)
    row_step = lax.broadcasted_iota(jnp.int32, (1, STRIP, 1), 1) * RATIO

    def accumulate(carry, item):
        piece, begin = item
        offset = point - begin[:, None, None]
        hat = jnp.maximum(RATIO - jnp.abs(offset - row_step), 0)
        hat = (
            jnp.where((offset >= 0) & (offset < STRIP * RATIO), hat, 0).astype(jnp.float32) / RATIO
        )
        return (carry + jnp.einsum("gat,gtp->ap", piece, hat, precision=top_wavenumber_kept), None)

    boundary = lax.scan(
        accumulate, jnp.zeros((fields * levels, NB), jnp.float32), (pieces, starts)
    )[0]
    return (advanced_state, boundary.reshape(1, fields, levels, NB))


def solution(mesh):
    return jax.shard_map(
        local,
        mesh=mesh,
        in_specs=(
            P(None, None, "lon", "lat"),
            P(None, "lat"),
            P(),
            P(),
            P(("lat", "lon"), None),
            P(("lat", "lon"), None, None),
        ),
        out_specs=(P(None, None, "lon", "lat"), P(("lat", "lon"), None, None, None)),
        check_vma=False,
    )
```

profile of v0, /device:TPU:1, one launch (start us, length us, event | category | flops | bytes accessed | tf_op | source)
XLA Modules:
  0.0 498.6 jit_solution(17846621195158147542)
XLA Ops:
  27.1 19.1 %copy.158 = f32[5,4,56,256]{0,1,2,3:T(4,128)} copy(f32[5,4,56,256]{3,0,2,1:T(8,128)S(1)} %fusion.42) | data formatting | bytes 2293760 | tf_op jit(solution)/shard_map/add | solution.py:88
  46.2 12.7 %gather_fusion = f32[64,5,4,16]{1,2,3,0:T(4,128)} fusion(f32[5,4,56,256]{0,1,2,3:T(4,128)} %copy.158, s32[64]{0:T(128)S(1)} %get-tuple-element.93), kind=kCustom, calls=%fused_computation | custom fusion | bytes 164864 | tf_op jit(solution)/shard_map/vmap()/gather | solution.py:110
  62.5 10.5 %all-to-all-start.2 = ((f32[64,2,320]{2,1,0:T(2,128)}), f32[64,2,320]{2,1,0:T(2,128)S(1)}, u32[]{:S(2)}, u32[]{:S(2)}) async-start(f32[64,2,320]{2,1,0:T(2,128)} %copy.161), calls=%async_computation.2 | async-start | bytes 393216 | tf_op jit(solution)/shard_map/all_to_all | solution.py:130
  94.1 15.4 %all-to-all-done = f32[64,1,2240]{2,1,0:T(1,128)} async-done(((f32[64,1,2240]{2,1,0:T(1,128)}), f32[64,1,2240]{2,1,0:T(1,128)}, u32[]{:S(2)}, u32[]{:S(2)}) %all-to-all-start) | async-done | bytes 573472 | tf_op jit(solution)/shard_map/all_to_all | solution.py:64
  118.2 18.5 %fusion.154 = f32[5,4,2,128]{3,0,2,1:T(8,128)S(1)} fusion(f32[5,4,2,3584]{3,0,2,1:T(8,128)} %reshape.513, f32[2,128]{1,0:T(2,128)S(1)} %get-tuple-element.103), kind=kOutput, calls=%fused_computation.165 | convolution fusion | flops 224334848 | bytes 594944 | tf_op jit(solution)/shard_map/flrn,nk->flrk/dot_general | solution.py:46
  154.1 9.0 %fusion.163 = f32[5,4,2,128]{3,0,2,1:T(8,128)S(1)} fusion(f32[5,4,2,3584]{3,0,2,1:T(8,128)S(1)} %copy-done.5, s32[128]{0:T(128)S(1)} %get-tuple-element.117, f32[2,128]{1,0:T(2,128)S(1)} %get-tuple-element.98), kind=kOutput, calls=%fused_computation.168 | convolution fusion | flops 224334848 | bytes 595456 | tf_op jit(solution)/shard_map/flrn,nk->flrk/dot_general | solution.py:49
  189.1 9.0 %fusion.175 = f32[5,4,2,128]{3,0,2,1:T(8,128)S(1)} fusion(f32[5,4,2,3584]{3,0,2,1:T(8,128)S(1)} %copy-done.5, s32[128]{0:T(128)S(1)} %get-tuple-element.115, f32[2,128]{1,0:T(2,128)S(1)} %get-tuple-element.100), kind=kOutput, calls=%fused_computation.172 | convolution fusion | flops 224334848 | bytes 595456 | tf_op jit(solution)/shard_map/flrn,nk->flrk/dot_general | solution.py:49
  224.2 9.0 %fusion.187 = f32[5,4,2,128]{3,0,2,1:T(8,128)S(1)} fusion(f32[5,4,2,3584]{3,0,2,1:T(8,128)S(1)} %copy-done.5, s32[128]{0:T(128)S(1)} %get-tuple-element.113, f32[2,128]{1,0:T(2,128)S(1)} %get-tuple-element.102), kind=kOutput, calls=%fused_computation.176 | convolution fusion | flops 224334848 | bytes 595456 | tf_op jit(solution)/shard_map/flrn,nk->flrk/dot_general | solution.py:49
  250.5 11.1 %fusion.87 = f32[5,4,2,3584]{3,0,2,1:T(8,128)S(1)} fusion(f32[5,4,2,128]{3,0,2,1:T(8,128)S(1)} %fusion.154), kind=kOutput, calls=%fused_computation.119 | convolution fusion | flops 224329728 | bytes 593920 | tf_op jit(solution)/shard_map/flrk,nk->flrn/dot_general | solution.py:53
  261.7 11.4 %convolution_add_fusion.12 = f32[5,4,2,3584]{3,0,2,1:T(8,128)S(1)} fusion(f32[5,4,2,3584]{3,0,2,1:T(8,128)S(1)} %fusion.87, f32[5,4,2,128]{3,0,2,1:T(8,128)S(1)} %fusion.157), kind=kOutput, calls=%fused_computation.39 | convolution fusion | flops 224473088 | bytes 1167360 | tf_op jit(solution)/shard_map/flrk,nk->flrn/dot_general | solution.py:54
  281.7 9.1 %convolution_add_fusion.10 = f32[5,4,2,3584]{3,0,2,1:T(8,128)S(1)} fusion(f32[5,4,2,3584]{3,0,2,1:T(8,128)S(1)} %convolution_add_fusion.11, f32[5,4,2,128]{3,0,2,1:T(8,128)S(1)} %fusion.163, s32[128]{0:T(128)S(1)} %get-tuple-element.117), kind=kOutput, calls=%fused_computation.37 | convolution fusion | flops 224473088 | bytes 1167872 | tf_op jit(solution)/shard_map/flrk,nk->flrn/dot_general | solution.py:54
  290.8 8.8 %convolution_add_fusion.9 = f32[5,4,2,3584]{3,0,2,1:T(8,128)S(1)} fusion(f32[5,4,2,3584]{3,0,2,1:T(8,128)S(1)} %convolution_add_fusion.10, f32[5,4,2,128]{3,0,2,1:T(8,128)S(1)} %fusion.166, s32[128]{0:T(128)S(1)} %get-tuple-element.116), kind=kOutput, calls=%fused_computation.36 | convolution fusion | flops 224473088 | bytes 1167872 | tf_op jit(solution)/shard_map/flrk,nk->flrn/dot_general | solution.py:53
  299.7 8.9 %convolution_add_fusion.8 = f32[5,4,2,3584]{3,0,2,1:T(8,128)S(1)} fusion(f32[5,4,2,3584]{3,0,2,1:T(8,128)S(1)} %convolution_add_fusion.9, f32[5,4,2,128]{3,0,2,1:T(8,128)S(1)} %fusion.169, s32[128]{0:T(128)S(1)} %get-tuple-element.116), kind=kOutput, calls=%fused_computation.35 | convolution fusion | flops 224473088 | bytes 1167872 | tf_op jit(solution)/shard_map/flrk,nk->flrn/dot_general | solution.py:54
  317.3 9.1 %convolution_add_fusion.6 = f32[5,4,2,3584]{3,0,2,1:T(8,128)S(1)} fusion(f32[5,4,2,3584]{3,0,2,1:T(8,128)S(1)} %convolution_add_fusion.7, f32[5,4,2,128]{3,0,2,1:T(8,128)S(1)} %fusion.175, s32[128]{0:T(128)S(1)} %get-tuple-element.115), kind=kOutput, calls=%fused_computation.33 | convolution fusion | flops 224473088 | bytes 1167872 | tf_op jit(solution)/shard_map/flrk,nk->flrn/dot_general | solution.py:54
  326.4 8.8 %convolution_add_fusion.5 = f32[5,4,2,3584]{3,0,2,1:T(8,128)S(1)} fusion(f32[5,4,2,3584]{3,0,2,1:T(8,128)S(1)} %convolution_add_fusion.6, f32[5,4,2,128]{3,0,2,1:T(8,128)S(1)} %fusion.178, s32[128]{0:T(128)S(1)} %get-tuple-element.114), kind=kOutput, calls=%fused_computation.32 | convolution fusion | flops 224473088 | bytes 1167872 | tf_op jit(solution)/shard_map/flrk,nk->flrn/dot_general | solution.py:53
  335.2 8.9 %convolution_add_fusion.4 = f32[5,4,2,3584]{3,0,2,1:T(8,128)S(1)} fusion(f32[5,4,2,3584]{3,0,2,1:T(8,128)S(1)} %convolution_add_fusion.5, f32[5,4,2,128]{3,0,2,1:T(8,128)S(1)} %fusion.181, s32[128]{0:T(128)S(1)} %get-tuple-element.114), kind=kOutput, calls=%fused_computation.31 | convolution fusion | flops 224473088 | bytes 1167872 | tf_op jit(solution)/shard_map/flrk,nk->flrn/dot_general | solution.py:54
  352.8 9.1 %convolution_add_fusion.2 = f32[5,4,2,3584]{3,0,2,1:T(8,128)S(1)} fusion(f32[5,4,2,3584]{3,0,2,1:T(8,128)S(1)} %convolution_add_fusion.3, f32[5,4,2,128]{3,0,2,1:T(8,128)S(1)} %fusion.187, s32[128]{0:T(128)S(1)} %get-tuple-element.113), kind=kOutput, calls=%fused_computation.29 | convolution fusion | flops 224473088 | bytes 1167872 | tf_op jit(solution)/shard_map/flrk,nk->flrn/dot_general | solution.py:54
  361.9 8.8 %convolution_add_fusion.1 = f32[5,4,2,3584]{3,0,2,1:T(8,128)S(1)} fusion(f32[5,4,2,3584]{3,0,2,1:T(8,128)S(1)} %convolution_add_fusion.2, f32[5,4,2,128]{3,0,2,1:T(8,128)S(1)} %fusion.190, s32[128]{0:T(128)S(1)} %get-tuple-element.112), kind=kOutput, calls=%fused_computation.28 | convolution fusion | flops 224473088 | bytes 1167872 | tf_op jit(solution)/shard_map/flrk,nk->flrn/dot_general | solution.py:53
  370.7 9.0 %convolution_add_fusion = f32[5,4,2,3584]{3,0,2,1:T(8,128)S(1)} fusion(f32[5,4,2,3584]{3,0,2,1:T(8,128)S(1)} %convolution_add_fusion.1, f32[5,4,2,128]{3,0,2,1:T(8,128)S(1)} %fusion.193, s32[128]{0:T(128)S(1)} %get-tuple-element.112), kind=kOutput, calls=%fused_computation.27 | convolution fusion | flops 224473088 | bytes 1167872 | tf_op jit(solution)/shard_map/flrk,nk->flrn/dot_general | solution.py:54
  379.8 14.3 %copy.154 = f32[5,4,2,3584]{0,2,1,3:T(2,128)} copy(f32[5,4,2,3584]{3,0,2,1:T(8,128)S(1)} %convolution_add_fusion) | data formatting | bytes 1146880 | tf_op jit(solution)/shard_map/add | solution.py:52
  394.1 18.6 %reshape.516 = f32[64,1,2240]{2,1,0:T(1,128)} reshape(f32[3584,4,2,5]{3,2,1,0:T(2,128)} %bitcast.215) | data formatting | bytes 1146880
  418.5 24.4 %while.11 = (s32[]{:T(128)}, f32[20,2048]{1,0:T(8,128)S(1)}, f32[8,16,20,16]{2,3,1,0:T(8,128)}, s32[8,16]{1,0:T(8,128)S(1)}, s32[]{:T(128)}, /*index=5*/s32[]{:T(128)}) while((s32[]{:T(128)}, f32[20,2048]{1,0:T(8,128)S(1)}, f32[8,16,20,16]{2,3,1,0:T(8,128)}, s32[8,16]{1,0:T(8,128)S(1)}, s32[]{:T(128)}, /*index=5*/s32[]{:T(128)}) %tuple.56), condition=%wide.region_2.3_spmd.clone, body=%wide.region_1.2_spmd.clone.sunk | while | flops 129744912 | bytes 787411 | solution.py:147
  445.6 24.6 %reshape.517 = f32[3584,4,2,5]{3,2,1,0:T(2,128)} reshape(f32[64,2240]{1,0:T(8,128)S(1)} %reduce.1) | data formatting | bytes 1146880
  470.2 21.4 %copy.183 = f32[5,4,2,64,56]{4,3,2,1,0:T(8,128)} copy(f32[5,4,2,64,56]{0,2,1,4,3:T(2,128)} %bitcast.216) | data formatting | bytes 1146880 | tf_op jit(solution)/shard_map/all_to_all | solution.py:62
  (137 shorter events, 211.3 us)
Async XLA Ops:
  0.6 18.4 %copy-start = (f32[4,5,5]{2,0,1:T(4,128)S(1)}, f32[4,5,5]{2,0,1:T(4,128)}, u32[]{:S(2)}) copy-start(f32[4,5,5]{2,0,1:T(4,128)} %param.10) | copy-start | bytes 1204
  0.6 6.0 %copy-start.3 = (f32[5,4,56,256]{3,2,1,0:T(8,128)S(1)}, f32[5,4,56,256]{3,2,1,0:T(8,128)}, u32[]{:S(2)}) copy-start(f32[5,4,56,256]{3,2,1,0:T(8,128)} %param.8) | copy-start | bytes 3440644
  0.7 5.7 %copy-start.9 = (f32[2,256]{1,0:T(2,128)S(1)}, f32[2,256]{1,0:T(2,128)}, u32[]{:S(2)}) copy-start(f32[2,256]{1,0:T(2,128)} %param.9) | copy-start | bytes 6148
  0.7 5.7 %copy-start.8 = (s32[64,4]{0,1:T(4,128)S(1)}, s32[64,4]{0,1:T(4,128)}, u32[]{:S(2)}) copy-start(s32[64,4]{0,1:T(4,128)} %param.12) | copy-start | bytes 3076
  2.4 4.9 collective-permute-start
  4.9 2.9 collective-permute-start.1
  7.4 2.6 copy-start.2
  9.1 9.9 %copy-start.4 = (f32[5,4,56,1]{3,0,2,1:T(8,128)S(1)}, f32[5,4,56,1]{3,0,2,1:T(8,128)}, u32[]{:S(2)}) copy-start(f32[5,4,56,1]{3,0,2,1:T(8,128)} %copy.128) | copy-start | bytes 13444
  10.0 4.7 collective-permute-start.2
  13.3 5.6 %collective-permute-start.3 = (f32[5,4,1,258]{3,0,2,1:T(8,128)S(1)}, f32[5,4,1,258]{3,0,2,1:T(8,128)S(1)}, u32[]{:S(2)}, u32[]{:S(2)}) collective-permute-start(f32[5,4,1,258]{3,0,2,1:T(8,128)S(1)} %get-tuple-element.89), channel_id=1, source_target_pairs={{0,1},{1,2},{2,3},{3,4},{4,5},{5,6},{6,7},{7,8},{8,9},{9,10},{10,1... | collective-permute-start | bytes 61928 | tf_op jit(solution)/shard_map/ppermute | solution.py:22
  62.5 22.6 %all-to-all-start.2 = ((f32[64,2,320]{2,1,0:T(2,128)}), f32[64,2,320]{2,1,0:T(2,128)S(1)}, u32[]{:S(2)}, u32[]{:S(2)}) async-start(f32[64,2,320]{2,1,0:T(2,128)} %copy.161), calls=%async_computation.2 | async-start | bytes 393216 | tf_op jit(solution)/shard_map/all_to_all | solution.py:130
  75.7 14.6 %copy-start.10 = (s32[1,64,2]{1,2,0:T(2,128)S(1)}, s32[1,64,2]{1,2,0:T(2,128)}, u32[]{:S(2)}) copy-start(s32[1,64,2]{1,2,0:T(2,128)} %param.13) | copy-start | bytes 1540
  75.7 14.8 %copy-start.11 = (s32[256]{0:T(256)S(1)}, s32[256]{0:T(256)}, u32[]{:S(2)}) copy-start(s32[256]{0:T(256)} %param.11) | copy-start | bytes 3076
  85.1 5.6 %copy-start.6 = (f32[64,2,320]{2,1,0:T(2,128)}, f32[64,2,320]{2,1,0:T(2,128)S(1)}, u32[]{:S(2)}) copy-start(f32[64,2,320]{2,1,0:T(2,128)S(1)} %all-to-all-done.2) | copy-start | bytes 491524
  85.1 24.3 %all-to-all-start = ((f32[64,1,2240]{2,1,0:T(1,128)}), f32[64,1,2240]{2,1,0:T(1,128)}, u32[]{:S(2)}, u32[]{:S(2)}) async-start(f32[64,1,2240]{2,1,0:T(1,128)} %reshape.514), calls=%async_computation | async-start | bytes 1179648 | tf_op jit(solution)/shard_map/all_to_all | solution.py:64
  118.2 18.5 %copy-start.5 = (f32[5,4,2,3584]{3,0,2,1:T(8,128)S(1)}, f32[5,4,2,3584]{3,0,2,1:T(8,128)}, u32[]{:S(2)}) copy-start(f32[5,4,2,3584]{3,0,2,1:T(8,128)} %reshape.513) | copy-start | bytes 1720324
  394.1 24.4 %copy-start.7 = (f32[20,2048]{1,0:T(8,128)S(1)}, f32[20,2048]{1,0:T(8,128)}, u32[]{:S(2)}) copy-start(f32[20,2048]{1,0:T(8,128)} %custom-call.2) | copy-start | bytes 491524
  412.7 30.9 %all-to-all-start.1 = ((f32[64,1,2240]{2,1,0:T(1,128)}), f32[64,1,2240]{2,1,0:T(1,128)S(1)}, u32[]{:S(2)}, u32[]{:S(2)}) async-start(f32[64,1,2240]{2,1,0:T(1,128)} %reshape.516), calls=%async_computation.1 | async-start | bytes 1179648 | tf_op jit(solution)/shard_map/all_to_all | solution.py:62
  495.5 2.7 copy-start.1
where the time goes:
time: 508 us; the launch traced here: 499 us
  matrix products  292 us (57%)
  local copies, waits for them, and re-layouts  138 us (27%)
  starting transfers between devices  28.6 us (6%)
  waiting for transfers between devices  27.7 us (5%)
  other arithmetic  9.93 us (2%)
    dot_general x7, matrix products, spectral_filter(): jnp.einsum('flrn,nk->flrk', rows, cosine, precision=top_wavenumber_kept)  70.5 us
    dot_general x7, matrix products, spectral_filter(): jnp.einsum('flrk,nk->flrn', imaginary_component, sine, precision=top_wave...  65.5 us
    dot_general x7, matrix products, spectral_filter(): jnp.einsum('flrk,nk->flrn', real_part, cosine, precision=top_wavenumber_k...  63.6 us
    dot_general x7, matrix products, spectral_filter(): jnp.einsum('flrn,nk->flrk', rows, sine, precision=top_wavenumber_kept)  61.7 us
    unnamed x34, local copies, waits for them, and re-layouts  52.5 us
    all_to_all x3, local copies, waits for them, and re-layouts, polar_pass(): lax.all_to_all(spectral_filter(lax.all_to_all(work_rows, 'lon', split_axi...  25.3 us
    dot_general x8, matrix products, accumulate(): jnp.einsum('gat,gtp->ap', piece, hat, precision=top_wavenumber_kept)  22.5 us
    add x1, local copies, waits for them, and re-layouts, local(): model_state + diffusion[0] * (east_west - 2.0 * model_state)  19.1 us
  transfers between devices with their start and end apart: 7, of which 4 were waited for; matrix products, arithmetic and copies ran while one was open for 7% of the time, Pallas kernels for 0%

commit v1 on v0

v1 whole, which is shorter than its diff:
```python
import jax
import jax.numpy as jnp
import ml_dtypes
import numpy as np
from jax import lax
from jax.experimental import pallas as pl
from jax.experimental.pallas import tpu as pltpu
from jax.sharding import PartitionSpec as P

MESH = pl.DeviceIdType.MESH
F32, BF16 = jnp.float32, jnp.bfloat16
FIELDS, LEVELS, COLS, ROWS = 5, 4, 56, 256
NLON, NDEV, POLAR, NB, RATIO, STRIP = 3584, 64, 128, 2048, 11, 16
PAIRS = FIELDS * LEVELS // 2
QROWS = 40
K1 = 28
CHUNKS = 4


def hi_lo(table):
    hi = table.astype(np.float32).astype(ml_dtypes.bfloat16)
    lo = (table - hi.astype(np.float64)).astype(np.float32).astype(ml_dtypes.bfloat16)
    return hi, lo


def tables():
    q = np.arange(QROWS)
    live = (q <= 32).astype(np.float64)
    c = np.arange(NDEV)
    lane = np.arange(128)
    unit, mu = lane // 64, lane % 64
    m = np.where(mu == 57, -1, mu)
    live_in = (mu <= 57).astype(np.float64)
    live_out = (mu < COLS).astype(np.float64)
    turn = 2 * np.pi * np.outer(q, c) / NDEV
    c1 = np.concatenate([np.cos(turn) * live[:, None], -np.sin(turn) * live[:, None]], 0)
    weight = np.where((q == 0) | (q == 32), 1.0, 2.0) * live / NLON
    c2 = np.concatenate([np.cos(turn) * weight[:, None], -np.sin(turn) * weight[:, None]], 0).T
    phi = 2 * np.pi * np.outer(q, m) / NLON
    twiddle = np.stack([np.cos(phi), np.sin(phi)]) * live[None, :, None]
    out = np.arange(128)
    unit_k, part_k, j = out // 64, (out % 64) // 32, out % 32
    k1 = j - 14
    live_k = (j < K1).astype(np.float64)
    psi = 2 * np.pi * np.outer(m, k1) / COLS
    same = (unit[:, None] == unit_k[None, :]) * live_k[None, :]
    cos, sin = np.cos(psi) * same, np.sin(psi) * same
    real = part_k[None, :] == 0
    b1 = np.concatenate([np.where(real, cos, -sin), np.where(real, sin, cos)], 0)
    b1 = b1 * np.tile(live_in, 2)[:, None]
    b2 = np.concatenate([np.where(real, cos, -sin).T, np.where(real, sin, cos).T], 1)
    b2 = b2 * np.tile(live_out, 2)[None, :]
    wave = np.abs(q[:, None] + 64 * k1[None, :])
    wave = np.where((live[:, None] > 0) & (live_k[None, :] > 0), wave, 1 << 20).astype(np.int32)

    def left(t):
        hi, lo = hi_lo(t)
        return np.concatenate([hi, hi, lo], 1)

    def right(t):
        hi, lo = hi_lo(t)
        return np.concatenate([hi, hi, lo], 0)

    return left(c1), twiddle.astype(np.float32), right(b1), wave, right(b2), left(c2)


def split(x):
    hi = x.astype(BF16)
    return hi, (x - hi.astype(F32)).astype(BF16)


def iota(shape, dim):
    return lax.broadcasted_iota(jnp.int32, shape, dim)


def dot(a, b):
    return jnp.dot(a, b, preferred_element_type=F32)


def place_of(device):
    return lax.rem(device, CHUNKS) * (NDEV // CHUNKS) + lax.div(device, CHUNKS)


def step_kernel(
    ms, dif, coup, cut, sl, npl, c1, tw, b1, wave, b2, c2,
    out, nest,
    pk, rl, arr, res, ret, zb, sn, ss, hw, he, hn, hs, xs, sb, rb, tb, lb,
    s_rel, r_rel, s_fwd, r_fwd, s_ret, r_ret, s_nest, r_nest, s_halo, r_halo,
):
    la, me = lax.axis_index("lat"), lax.axis_index("lon")
    polar_lat = jnp.where(la < 2, 0, 3)
    helper_lat = jnp.where(la < 2, 1, 2)
    is_polar = la == polar_lat
    is_helper = jnp.logical_not(is_polar)
    half = jnp.where(is_polar, 0, 1)
    start = pl.multiple_of(jnp.where(la == 3, ROWS - POLAR, 0), 128)
    has_north, has_south = la > 0, la < 3
    mine = place_of(me)

    def remote(src, dst, s, r, lat, lon):
        return pltpu.make_async_remote_copy(
            src, dst, s, r, device_id={"lat": lat, "lon": lon}, device_id_type=MESH
        )

    barrier = pltpu.get_barrier_semaphore()

    def greet(lat, lon):
        pl.semaphore_signal(barrier, device_id={"lat": lat, "lon": lon}, device_id_type=MESH)

    @pl.when(has_north)
    def _():
        greet(la - 1, me)

    @pl.when(has_south)
    def _():
        greet(la + 1, me)

    def greet_plane(k, carry):
        greet(la, lax.rem(me + k, NDEV))
        return carry

    lax.fori_loop(1, NDEV, greet_plane, 0)

    d0, d1 = dif[0:1, :], dif[1:2, :]
    lane_row = iota((COLS, ROWS), 1)
    col = iota((COLS, ROWS), 0)
    lane_u = iota((COLS, 128), 1)
    sn[...] = jnp.zeros_like(sn)
    ss[...] = jnp.zeros_like(ss)

    def level(l, carry):
        x = [ms[g, l] for g in range(FIELDS)]
        for f in range(FIELDS):
            own = x[f]
            east = jnp.where(col == COLS - 1, 0.0, pltpu.roll(own, COLS - 1, 0))
            west = jnp.where(col == 0, 0.0, pltpu.roll(own, 1, 0))
            south = jnp.where(lane_row == ROWS - 1, 0.0, pltpu.roll(own, ROWS - 1, 1))
            north = jnp.where(lane_row == 0, 0.0, pltpu.roll(own, 1, 1))
            acc = own + d0 * (east + west - 2.0 * own) + d1 * (north + south - 2.0 * own)
            for g in range(FIELDS):
                acc = acc + coup[l, f, g] * x[g]
            out[f, l] = acc
            u = f * LEVELS + l
            sn[...] = jnp.where(lane_u == u, own[:, 0:1], sn[...])
            ss[...] = jnp.where(lane_u == u, own[:, ROWS - 1 : ROWS], ss[...])
        return carry

    lax.fori_loop(0, LEVELS, level, 0)

    @pl.when(is_polar)
    def _():
        tail_row = iota((8, 128), 0)
        d0p = dif[0:1, pl.ds(start, POLAR)]

        def pack(k, carry):
            f, l0 = lax.div(k, 2), 2 * lax.rem(k, 2)
            rows = []
            for p in range(2):
                first = ms[f, l0 + p, 0:1, pl.ds(start, POLAR)]
                last = ms[f, l0 + p, COLS - 1 : COLS, pl.ds(start, POLAR)]
                tail = jnp.where(tail_row == 0, last, jnp.where(tail_row == 1, first, 0.0)) * d0p
                rows += [out[f, l0 + p, :, pl.ds(start, POLAR)], tail]
            turned = jnp.concatenate(rows, 0).T
            pk[k, 0] = turned[:NDEV]
            pk[k, 1] = turned[NDEV:]
            return carry

        lax.fori_loop(0, PAIRS, pack, 0)

    pl.semaphore_wait(barrier, NDEV - 1 + jnp.where(is_polar, 1, 2))

    east_dev, west_dev = lax.rem(me + 1, NDEV), lax.rem(me + NDEV - 1, NDEV)
    to_east = remote(ms.at[:, :, pl.ds(COLS - 1, 1)], hw, s_halo.at[0], r_halo.at[0], la, east_dev)
    to_west = remote(ms.at[:, :, pl.ds(0, 1)], he, s_halo.at[1], r_halo.at[1], la, west_dev)
    to_south = remote(ss, hn, s_halo.at[2], r_halo.at[2], jnp.minimum(la + 1, 3), me)
    to_north = remote(sn, hs, s_halo.at[3], r_halo.at[3], jnp.maximum(la - 1, 0), me)

    size = NDEV // CHUNKS

    def relay(g):
        rows = pl.ds(g * size, size)
        return remote(pk.at[:, 1, rows], rl.at[:, rows], s_rel.at[g], r_rel.at[g], helper_lat, me)

    @pl.when(is_polar)
    def _():
        for g in range(CHUNKS):
            relay(g).start()

    to_east.start()
    to_west.start()
    pl.when(has_south)(to_south.start)
    pl.when(has_north)(to_north.start)

    @pl.when(is_polar)
    def _():
        pltpu.make_async_copy(pk.at[:, 0, mine], arr.at[:, me], r_fwd).start()

        def send(k, carry):
            d = lax.rem(me + k, NDEV)
            remote(pk.at[:, 0, place_of(d)], arr.at[:, me], s_fwd, r_fwd, la, d).start()
            return carry

        lax.fori_loop(1, NDEV, send, 0)

    @pl.when(is_helper)
    def _():
        for g in range(CHUNKS):
            relay(g).wait_recv()

            def send(i, carry, g=g):
                b = lax.rem(i + lax.div(me, CHUNKS), size)
                d = b * CHUNKS + g

                @pl.when(d != me)
                def _():
                    remote(rl.at[:, g * size + b], arr.at[:, me], s_fwd, r_fwd, la, d).start()

                return carry

            lax.fori_loop(0, size, send, 0)
        pltpu.make_async_copy(rl.at[:, mine], arr.at[:, me], r_fwd).start()

    to_east.wait_recv()
    to_west.wait_recv()
    for f in range(FIELDS):
        for l in range(LEVELS):
            out[f, l, 0:1] += d0 * hw[f, l]
            out[f, l, COLS - 1 : COLS] += d0 * he[f, l]

    @pl.when(has_north)
    def _():
        to_south.wait_recv()
        halo = hn[...]
        d = dif[1:2, 0:128]

        def fix(u, carry):
            f, l = lax.div(u, LEVELS), lax.rem(u, LEVELS)
            value = pltpu.roll(halo, lax.rem(128 - u, 128), 1)
            out[f, l, :, 0:128] += jnp.where(lane_u == 0, d * value, 0.0)
            return carry

        lax.fori_loop(0, FIELDS * LEVELS, fix, 0)

    @pl.when(has_south)
    def _():
        to_north.wait_recv()
        halo = hs[...]
        d = dif[1:2, 128:256]

        def fix(u, carry):
            f, l = lax.div(u, LEVELS), lax.rem(u, LEVELS)
            value = pltpu.roll(halo, 127 - u, 1)
            out[f, l, :, 128:256] += jnp.where(lane_u == 127, d * value, 0.0)
            return carry

        lax.fori_loop(0, FIELDS * LEVELS, fix, 0)

    owners = sl[:, 0:1].astype(F32)
    columns, offsets, lengths = sl[:, 1:2], sl[:, 2:3], sl[:, 3:4]
    eye = iota((NDEV, NDEV), 0) == iota((NDEV, NDEV), 1)
    owner_row = jnp.sum(jnp.where(eye, owners, 0.0), axis=0, keepdims=True)
    before = (owners == owner_row) & (iota((NDEV, NDEV), 1) < iota((NDEV, NDEV), 0))
    rank = jnp.sum(jnp.where(before, 1.0, 0.0), axis=1, keepdims=True)
    slot = rank * NDEV + owners
    twice = iota((NDEV, 128), 0) == lax.rem(iota((NDEV, 128), 1), NDEV)
    slot_row = jnp.sum(jnp.where(twice, slot, 0.0), axis=0, keepdims=True)
    routing = jnp.where(iota((128, 128), 0).astype(F32) == slot_row, 1.0, 0.0).astype(BF16)
    pick = jnp.where(lax.rem(iota((NDEV, 128), 1), NDEV) == columns, 1.0, 0.0).astype(BF16)
    high = offsets >= 128
    inner = lax.rem(offsets, 128)
    lane = iota((NDEV, 128), 1)
    spill = (lane < STRIP) & (inner > 128 - STRIP)
    bits = lax.div(inner, 1)
    zero8 = jnp.zeros((8, ROWS), F32)

    def strips_of(u, carry):
        x = out[lax.div(u, LEVELS), lax.rem(u, LEVELS)]
        top = x.astype(BF16).astype(F32)
        y = dot(pick, jnp.concatenate([top, zero8, x - top, zero8], 0).astype(BF16))
        a = jnp.where(high, y[:, 128:], y[:, :128])
        a = jnp.where(spill, y[:, 128:], a)
        for shift in (64, 32, 16):
            a = jnp.where((bits & shift) != 0, pltpu.roll(a, 128 - shift, 1), a)
        xs[u] = a
        return carry

    lax.fori_loop(0, FIELDS * LEVELS, strips_of, 0)
    window = lax.div(lane, 32)
    for g in range(3):
        both = []
        for h in range(2):
            a = jnp.zeros((NDEV, 128), F32)
            for i in range(4):
                u = 8 * g + 2 * i + h
                if u < FIELDS * LEVELS:
                    v = xs[u] if i == 0 else pltpu.roll(xs[u], 32 * i, 1)
                    a = jnp.where(window == i, v, a)
            for shift in (8, 4, 2, 1):
                a = jnp.where((bits & shift) != 0, pltpu.roll(a, 128 - shift, 1), a)
            both.append(a)
        a = jnp.where(lax.rem(lane, 32) < 16, both[0], pltpu.roll(both[1], 16, 1))
        a = jnp.where(lax.rem(lane, STRIP) < lengths, a, 0.0)
        a = dot(routing, jnp.concatenate(split(a), 0))
        sb[g, 0] = a[:NDEV]
        sb[g, 1] = a[NDEV:]

    pltpu.make_async_copy(sb.at[:, :, me], rb.at[:, :, me], r_nest).start()

    def send_strips(k, carry):
        d = lax.rem(me + k, NDEV)
        remote(sb.at[:, :, d], rb.at[:, :, me], s_nest, r_nest, la, d).start()
        return carry

    lax.fori_loop(1, NDEV, send_strips, 0)

    pltpu.make_async_copy(arr, arr, r_fwd).wait()
    cos, sin = tw[0], tw[1]

    def forward(k, carry):
        hi, lo = split(arr[k])
        y = dot(c1[...], jnp.concatenate([hi, lo, hi], 0))
        re, im = y[:QROWS], y[QROWS:]
        zb[k, :, 0:128] = re * cos + im * sin
        zb[k, :, 128:256] = im * cos - re * sin
        return carry

    lax.fori_loop(0, PAIRS, forward, 0)
    hi, lo = split(zb[...].reshape(PAIRS * QROWS, 256))
    spectrum = dot(jnp.concatenate([hi, lo, hi], 1), b1[...])
    base = jnp.where(la < 2, 0, POLAR) + half * NDEV
    keep = wave[...] < cut[base + mine]
    spectrum = jnp.where(keep[None], spectrum.reshape(PAIRS, QROWS, 128), 0.0)
    hi, lo = split(spectrum.reshape(PAIRS * QROWS, 128))
    zb[...] = dot(jnp.concatenate([hi, lo, hi], 1), b2[...]).reshape(PAIRS, QROWS, 256)

    def backward(k, carry):
        re, im = zb[k, :, 0:128], zb[k, :, 128:256]
        turned = jnp.concatenate([re * cos - im * sin, re * sin + im * cos], 0)
        hi, lo = split(turned)
        res[k] = dot(c2[...], jnp.concatenate([hi, lo, hi], 0))
        return carry

    lax.fori_loop(0, PAIRS, backward, 0)

    @pl.when(is_polar)
    def _():
        pltpu.make_async_copy(res.at[:, me], ret.at[:, 0, mine], r_ret).start()

    @pl.when(is_helper)
    def _():
        remote(res.at[:, me], ret.at[:, 1, mine], s_ret, r_ret, polar_lat, me).start()

    def send_back(k, carry):
        d = lax.rem(me + k, NDEV)
        remote(res.at[:, d], ret.at[:, half, mine], s_ret, r_ret, polar_lat, d).start()
        return carry

    lax.fori_loop(1, NDEV, send_back, 0)

    pltpu.make_async_copy(rb, rb, r_nest).wait()
    for g in range(3):
        tb[g] = jnp.concatenate([rb[g, 0], rb[g, 1]], 0).T
    for t in range(STRIP):
        x = jnp.concatenate([tb[g, pl.ds(t, 8, stride=STRIP), :] for g in range(3)], 0)
        top = x.astype(BF16).astype(F32)
        lb[:, t * 128 : (t + 1) * 128] = jnp.concatenate([top, x - top], 0).astype(BF16)
    places = npl[0].astype(F32)
    lane_c = iota((NDEV, 128), 1)
    chosen = jnp.where(lane_c < NDEV, places[:, 0:1], places[:, 1:2])
    begin = jnp.sum(jnp.where(twice, chosen, 0.0), axis=0, keepdims=True)
    wide = 256
    point = iota((wide, 128), 0).astype(F32)

    def boundary(n, carry):
        first = pl.multiple_of(n * wide, wide)
        away = point + (n * wide).astype(F32) - begin
        hats = []
        for t in range(STRIP):
            d = away - float(RATIO * t)
            hat = jnp.maximum(float(RATIO) - jnp.abs(d), 0.0)
            if t == 0:
                hat = jnp.where(d >= 0.0, hat, 0.0)
            hats.append(hat.astype(BF16))
        total = lax.dot_general(
            lb[...], jnp.concatenate(hats, 1), (((1,), (1,)), ((), ())), preferred_element_type=F32
        )
        total = (total[:24] + total[24:]) * (1.0 / RATIO)
        for f in range(FIELDS):
            nest[0, f, :, pl.ds(first, wide)] = total[f * LEVELS : (f + 1) * LEVELS]
        return carry

    lax.fori_loop(0, NB // wide, boundary, 0)

    @pl.when(is_polar)
    def _():
        pltpu.make_async_copy(ret, ret, r_ret).wait()

        def unpack(k, carry):
            f, l0 = lax.div(k, 2), 2 * lax.rem(k, 2)
            turned = jnp.concatenate([ret[k, 0], ret[k, 1]], 0).T
            out[f, l0, :, pl.ds(start, POLAR)] = turned[:COLS]
            out[f, l0 + 1, :, pl.ds(start, POLAR)] = turned[64 : 64 + COLS]
            return carry

        lax.fori_loop(0, PAIRS, unpack, 0)

    to_east.wait_send()
    to_west.wait_send()
    pl.when(has_south)(to_south.wait_send)
    pl.when(has_north)(to_north.wait_send)
    others = pl.ds(0, NDEV - 1)
    pltpu.make_async_copy(res.at[:, others], res.at[:, others], s_fwd).wait()
    pltpu.make_async_copy(sb.at[:, :, others], sb.at[:, :, others], s_nest).wait()

    @pl.when(is_polar)
    def _():
        for g in range(CHUNKS):
            relay(g).wait_send()
        pltpu.make_async_copy(res.at[:, others], res.at[:, others], s_ret).wait()

    @pl.when(is_helper)
    def _():
        pltpu.make_async_copy(res, res, s_ret).wait()


def local(model_state, diffusion, coupling, cutoff, strip_list, nest_place):
    vmem = pl.BlockSpec(memory_space=pltpu.VMEM)
    smem = pl.BlockSpec(memory_space=pltpu.SMEM)
    dma = pltpu.SemaphoreType.DMA
    constants = [jnp.asarray(t) for t in tables()]
    return pl.pallas_call(
        step_kernel,
        name="dynamics_step",
        out_shape=[
            jax.ShapeDtypeStruct(model_state.shape, F32),
            jax.ShapeDtypeStruct((1, FIELDS, LEVELS, NB), F32),
        ],
        in_specs=[vmem, vmem, smem, smem, vmem, vmem] + [vmem] * len(constants),
        out_specs=[vmem, vmem],
        scratch_shapes=[
            pltpu.VMEM((PAIRS, 2, NDEV, 128), F32),
            pltpu.VMEM((PAIRS, NDEV, 128), F32),
            pltpu.VMEM((PAIRS, NDEV, 128), F32),
            pltpu.VMEM((PAIRS, NDEV, 128), F32),
            pltpu.VMEM((PAIRS, 2, NDEV, 128), F32),
            pltpu.VMEM((PAIRS, QROWS, 256), F32),
            pltpu.VMEM((COLS, 128), F32),
            pltpu.VMEM((COLS, 128), F32),
            pltpu.VMEM((FIELDS, LEVELS, 1, ROWS), F32),
            pltpu.VMEM((FIELDS, LEVELS, 1, ROWS), F32),
            pltpu.VMEM((COLS, 128), F32),
            pltpu.VMEM((COLS, 128), F32),
            pltpu.VMEM((FIELDS * LEVELS, NDEV, 128), F32),
            pltpu.VMEM((3, 2, NDEV, 128), F32),
            pltpu.VMEM((3, 2, NDEV, 128), F32),
            pltpu.VMEM((3, 128, 128), F32),
            pltpu.VMEM((48, STRIP * 128), BF16),
            dma((CHUNKS,)), dma((CHUNKS,)),
            dma, dma, dma, dma, dma, dma,
            dma((4,)), dma((4,)),
        ],
        compiler_params=pltpu.CompilerParams(
            collective_id=0, has_side_effects=True, vmem_limit_bytes=48 << 20
        ),
    )(model_state, diffusion, coupling, cutoff, strip_list, nest_place, *constants)


def solution(mesh):
    return jax.shard_map(
        local,
        mesh=mesh,
        in_specs=(
            P(None, None, "lon", "lat"),
            P(None, "lat"),
            P(),
            P(),
            P(("lat", "lon"), None),
            P(("lat", "lon"), None, None),
        ),
        out_specs=(P(None, None, "lon", "lat"), P(("lat", "lon"), None, None, None)),
        check_vma=False,
    )
```

time: 508 us -> 60.4 us (0.12); the launches traced: 499 us -> 59.9 us
  matrix products: 292 us -> 0 us
  local copies, waits for them, and re-layouts: 138 us -> 11.4 us
  Pallas kernels: 0 us -> 47.8 us
  starting transfers between devices: 28.6 us -> 0 us
  waiting for transfers between devices: 27.7 us -> 0 us
  other arithmetic: 9.93 us -> 0 us
    dot_general x38 -> x0, matrix products: 292 us -> none  [the longest x7 70.5 us: spectral_filter(): jnp.einsum('flrn,nk->flrk', rows, cosine, precision=top_wavenumber_kept)]
    pallas_call x0 -> x1, Pallas kernels: none -> 47.8 us  [local(): pl.pallas_call(step_kernel, name='dynamics_step', out_shape=[jax.ShapeDty...]
    unnamed x34 -> x23, local copies, waits for them, and re-layouts: 52.5 us -> 11.4 us
    add x2 -> x0, local copies, waits for them, and re-layouts: 33.4 us -> none  [the longest x1 19.1 us: local(): model_state + diffusion[0] * (east_west - 2.0 * model_state)]
    all_to_all x7 -> x0, local copies, waits for them, and re-layouts: 27.9 us -> none  [the longest x3 25.3 us: polar_pass(): lax.all_to_all(spectral_filter(lax.all_to_all(work_rows, 'lon', split_axi...]
    all_to_all x3 -> x0, waiting for transfers between devices: 22.1 us -> none  [the longest x1 15.4 us: polar_pass(): lax.all_to_all(work_rows, 'lon', split_axis=2, concat_axis=3, tiled=True)]
    all_to_all x3 -> x0, starting transfers between devices: 21.5 us -> none  [the longest x1 10.5 us: local(): lax.all_to_all(outgoing, 'lon', split_axis=0, concat_axis=0, tiled=True)]
    gather x2 -> x0, local copies, waits for them, and re-layouts: 15.1 us -> none  [cut_strip(): lax.dynamic_slice(updated, (zero, zero, column, offset), (fields, levels,...]
  transfers between devices with their start and end apart: 7 -> 0, of which waited for: 4 -> 0; matrix products, arithmetic and copies ran while one was open for 7% -> 0% of each run, Pallas kernels for 0% -> 0%
where the time goes in v1:
time: 60.4 us; the launch traced here: 59.9 us
  Pallas kernels  47.8 us (79%)
  local copies, waits for them, and re-layouts  11.4 us (19%)
  between operations  0.65 us (1%)
    pallas_call x1, Pallas kernels, local(): pl.pallas_call(step_kernel, name='dynamics_step', out_shape=[jax.ShapeDty...  47.8 us
    unnamed x23, local copies, waits for them, and re-layouts  11.4 us

profile of v1, /device:TPU:1, one launch (start us, length us, event | category | flops | bytes accessed | tf_op | source)
XLA Modules:
  0.0 59.9 jit_solution(2931957080005049117)
XLA Ops:
  0.6 0.7 %copy.14.coup = f32[4,5,5]{2,1,0:T(8,128)S(1)} copy(f32[4,5,5]{2,0,1:T(4,128)} %param.14) | data formatting | bytes 800 | tf_op args[2]
  1.3 0.8 %copy.15.sl = s32[64,4]{1,0:T(8,128)S(1)} copy(s32[64,4]{0,1:T(4,128)} %param.16) | data formatting | bytes 2048 | tf_op args[4]
  2.1 0.8 %copy.16.npl = s32[1,64,2]{2,1,0:T(8,128)S(1)} copy(s32[1,64,2]{1,2,0:T(2,128)} %param.17) | data formatting | bytes 1024 | tf_op args[5]
  2.9 0.0 copy-start
  2.9 1.3 %copy-done = f32[5,4,56,256]{3,2,1,0:T(8,128)S(1)} copy-done((f32[5,4,56,256]{3,2,1,0:T(8,128)S(1)}, f32[5,4,56,256]{3,2,1,0:T(8,128)}, u32[]{:S(2)}) %copy-start) | copy-done | bytes 1146904
  4.1 0.0 copy-start.1
  4.1 0.9 %copy-done.1 = bf16[384,256]{1,0:T(8,128)(2,1)S(1)} copy-done((bf16[384,256]{1,0:T(8,128)(2,1)S(1)}, bf16[384,256]{1,0:T(8,128)(2,1)}, u32[]{:S(2)}) %copy-start.1) | copy-done | bytes 196632
  5.1 0.0 copy-start.2
  5.1 0.9 %copy-done.2 = bf16[768,128]{1,0:T(8,128)(2,1)S(1)} copy-done((bf16[768,128]{1,0:T(8,128)(2,1)S(1)}, bf16[768,128]{1,0:T(8,128)(2,1)}, u32[]{:S(2)}) %copy-start.2) | copy-done | bytes 196632
  6.0 0.0 copy-start.3
  6.0 0.8 %copy-done.3 = f32[2,40,128]{2,1,0:T(8,128)S(1)} copy-done((f32[2,40,128]{2,1,0:T(8,128)S(1)}, f32[2,40,128]{2,1,0:T(8,128)}, u32[]{:S(2)}) %copy-start.3) | copy-done | bytes 40984
  6.8 0.0 copy-start.4
  6.8 0.8 %copy-done.4 = bf16[80,192]{1,0:T(8,128)(2,1)S(1)} copy-done((bf16[80,192]{1,0:T(8,128)(2,1)S(1)}, bf16[80,192]{1,0:T(8,128)(2,1)}, u32[]{:S(2)}) %copy-start.4) | copy-done | bytes 30744
  7.5 0.0 copy-start.5
  7.5 0.8 %copy-done.5 = bf16[64,240]{1,0:T(8,128)(2,1)S(1)} copy-done((bf16[64,240]{1,0:T(8,128)(2,1)S(1)}, bf16[64,240]{1,0:T(8,128)(2,1)}, u32[]{:S(2)}) %copy-start.5) | copy-done | bytes 30744
  8.3 0.0 copy-start.6
  8.3 0.7 %copy-done.6 = s32[40,128]{1,0:T(8,128)S(1)} copy-done((s32[40,128]{1,0:T(8,128)S(1)}, s32[40,128]{1,0:T(8,128)}, u32[]{:S(2)}) %copy-start.6) | copy-done | bytes 20504
  9.0 0.0 copy-start.7
  9.0 0.7 %copy-done.7 = f32[2,256]{1,0:T(2,128)S(1)} copy-done((f32[2,256]{1,0:T(2,128)S(1)}, f32[2,256]{1,0:T(2,128)}, u32[]{:S(2)}) %copy-start.7) | copy-done | bytes 2072
  9.7 0.0 copy-start.8
  9.7 0.7 %copy-done.8 = s32[256]{0:T(256)S(1)} copy-done((s32[256]{0:T(256)S(1)}, s32[256]{0:T(256)}, u32[]{:S(2)}) %copy-start.8) | copy-done | bytes 1048
  10.4 47.8 %dynamics_step.1 = (f32[5,4,56,256]{3,2,1,0:T(8,128)S(1)}, f32[1,5,4,2048]{3,2,1,0:T(4,128)S(1)}) custom-call(f32[5,4,56,256]{3,2,1,0:T(8,128)S(1)} %copy-done, f32[2,256]{1,0:T(2,128)S(1)} %copy-done.7, f32[4,5,5]{2,1,0:T(8,128)S(1)} %copy.14.coup, s32[256]{0:T(256)S(1)} %copy-done.8, s32[64,4]{1,0:T(8,128)S(1)} %copy.15.sl, s32[1,64,2]{2,1,0:T(8,128)S(1)} %copy.16.npl, ...), custom_call_target="tpu_custom_call" | custom-call | tf_op jit(solution)/shard_map/dynamics_step/pallas_call | solution.py:431
  58.2 1.0 %copy.19 = f32[5,4,56,256]{3,2,1,0:T(8,128)} copy(f32[5,4,56,256]{3,2,1,0:T(8,128)S(1)} %get-tuple-element.4) | data formatting | bytes 2293760
  59.2 0.7 %copy.20 = f32[1,5,4,2048]{3,2,1,0:T(4,128)} copy(f32[1,5,4,2048]{3,2,1,0:T(4,128)S(1)} %get-tuple-element.5) | data formatting | bytes 327680
Async XLA Ops:
  2.9 1.3 %copy-start = (f32[5,4,56,256]{3,2,1,0:T(8,128)S(1)}, f32[5,4,56,256]{3,2,1,0:T(8,128)}, u32[]{:S(2)}) copy-start(f32[5,4,56,256]{3,2,1,0:T(8,128)} %ms.1) | copy-start | bytes 3440644
  4.1 0.9 %copy-start.1 = (bf16[384,256]{1,0:T(8,128)(2,1)S(1)}, bf16[384,256]{1,0:T(8,128)(2,1)}, u32[]{:S(2)}) copy-start(bf16[384,256]{1,0:T(8,128)(2,1)} %constant.16.clone.b2) | copy-start | bytes 589828
  5.1 0.9 %copy-start.2 = (bf16[768,128]{1,0:T(8,128)(2,1)S(1)}, bf16[768,128]{1,0:T(8,128)(2,1)}, u32[]{:S(2)}) copy-start(bf16[768,128]{1,0:T(8,128)(2,1)} %constant.14.clone.b1) | copy-start | bytes 589828
  6.0 0.8 %copy-start.3 = (f32[2,40,128]{2,1,0:T(8,128)S(1)}, f32[2,40,128]{2,1,0:T(8,128)}, u32[]{:S(2)}) copy-start(f32[2,40,128]{2,1,0:T(8,128)} %constant.13.clone.tw) | copy-start | bytes 122884
  6.8 0.8 %copy-start.4 = (bf16[80,192]{1,0:T(8,128)(2,1)S(1)}, bf16[80,192]{1,0:T(8,128)(2,1)}, u32[]{:S(2)}) copy-start(bf16[80,192]{1,0:T(8,128)(2,1)} %constant.12.clone.c1) | copy-start | bytes 92164
  7.5 0.8 %copy-start.5 = (bf16[64,240]{1,0:T(8,128)(2,1)S(1)}, bf16[64,240]{1,0:T(8,128)(2,1)}, u32[]{:S(2)}) copy-start(bf16[64,240]{1,0:T(8,128)(2,1)} %constant.17.clone.c2) | copy-start | bytes 92164
  8.3 0.7 %copy-start.6 = (s32[40,128]{1,0:T(8,128)S(1)}, s32[40,128]{1,0:T(8,128)}, u32[]{:S(2)}) copy-start(s32[40,128]{1,0:T(8,128)} %constant.15.clone.wave) | copy-start | bytes 61444
  9.0 0.7 %copy-start.7 = (f32[2,256]{1,0:T(2,128)S(1)}, f32[2,256]{1,0:T(2,128)}, u32[]{:S(2)}) copy-start(f32[2,256]{1,0:T(2,128)} %dif.1) | copy-start | bytes 6148
  9.7 0.7 %copy-start.8 = (s32[256]{0:T(256)S(1)}, s32[256]{0:T(256)}, u32[]{:S(2)}) copy-start(s32[256]{0:T(256)} %cut.1) | copy-start | bytes 3076

commit v2 on v1

--- a/solution.py
+++ b/solution.py
@@ -50,9 +50,6 @@
     b1 = b1 * np.tile(live_in, 2)[:, None]
     b2 = np.concatenate([np.where(real, cos, -sin).T, np.where(real, sin, cos).T], 1)
     b2 = b2 * np.tile(live_out, 2)[None, :]
-    wave = np.abs(q[:, None] + 64 * k1[None, :])
-    wave = np.where((live[:, None] > 0) & (live_k[None, :] > 0), wave, 1 << 20).astype(np.int32)
-
     def left(t):
         hi, lo = hi_lo(t)
         return np.concatenate([hi, hi, lo], 1)
@@ -61,7 +58,7 @@
         hi, lo = hi_lo(t)
         return np.concatenate([hi, hi, lo], 0)
 
-    return left(c1), twiddle.astype(np.float32), right(b1), wave, right(b2), left(c2)
+    return left(c1), twiddle.astype(np.float32), right(b1), right(b2), left(c2)
 
 
 def split(x):
@@ -82,8 +79,9 @@
 
 
 def step_kernel(
-    ms, dif, coup, cut, sl, npl, c1, tw, b1, wave, b2, c2,
+    ms_hbm, dif_hbm, coup_hbm, cut_hbm, sl_hbm, npl_hbm, c1_hbm, tw_hbm, b1_hbm, b2_hbm, c2_hbm,
     out, nest,
+    ms, dif, coup, cut, sl, npl, c1, tw, b1, b2, c2, s_load,
     pk, rl, arr, res, ret, zb, sn, ss, hw, he, hn, hs, xs, sb, rb, tb, lb,
     s_rel, r_rel, s_fwd, r_fwd, s_ret, r_ret, s_nest, r_nest, s_halo, r_halo,
 ):
@@ -102,6 +100,13 @@
             src, dst, s, r, device_id={"lat": lat, "lon": lon}, device_id_type=MESH
         )
 
+    early = [(ms_hbm, ms), (dif_hbm, dif), (coup_hbm, coup)]
+    late = [(cut_hbm, cut), (sl_hbm, sl), (npl_hbm, npl), (c1_hbm, c1), (tw_hbm, tw)]
+    late += [(b1_hbm, b1), (b2_hbm, b2), (c2_hbm, c2)]
+    loads = [pltpu.make_async_copy(a, b, s_load.at[i]) for i, (a, b) in enumerate(early + late)]
+    for load in loads:
+        load.start()
+
     barrier = pltpu.get_barrier_semaphore()
 
     def greet(lat, lon):
@@ -120,6 +125,8 @@
         return carry
 
     lax.fori_loop(1, NDEV, greet_plane, 0)
+    for load in loads[: len(early)]:
+        load.wait()
 
     d0, d1 = dif[0:1, :], dif[1:2, :]
     lane_row = iota((COLS, ROWS), 1)
@@ -138,7 +145,7 @@
             north = jnp.where(lane_row == 0, 0.0, pltpu.roll(own, 1, 1))
             acc = own + d0 * (east + west - 2.0 * own) + d1 * (north + south - 2.0 * own)
             for g in range(FIELDS):
-                acc = acc + coup[l, f, g] * x[g]
+                acc = acc + coup[f, l, g] * x[g]
             out[f, l] = acc
             u = f * LEVELS + l
             sn[...] = jnp.where(lane_u == u, own[:, 0:1], sn[...])
@@ -220,6 +227,9 @@
             lax.fori_loop(0, size, send, 0)
         pltpu.make_async_copy(rl.at[:, mine], arr.at[:, me], r_fwd).start()
 
+    for load in loads[len(early) :]:
+        load.wait()
+
     to_east.wait_recv()
     to_west.wait_recv()
     for f in range(FIELDS):
@@ -255,10 +265,14 @@
 
         lax.fori_loop(0, FIELDS * LEVELS, fix, 0)
 
-    owners = sl[:, 0:1].astype(F32)
-    columns, offsets, lengths = sl[:, 1:2], sl[:, 2:3], sl[:, 3:4]
     eye = iota((NDEV, NDEV), 0) == iota((NDEV, NDEV), 1)
-    owner_row = jnp.sum(jnp.where(eye, owners, 0.0), axis=0, keepdims=True)
+
+    def upright(row):
+        return jnp.sum(jnp.where(eye, row.astype(F32), 0.0), axis=1, keepdims=True)
+
+    owner_row = sl[0:1, :].astype(F32)
+    owners = upright(owner_row)
+    columns, offsets, lengths = (upright(sl[i : i + 1, :]).astype(jnp.int32) for i in range(1, 4))
     before = (owners == owner_row) & (iota((NDEV, NDEV), 1) < iota((NDEV, NDEV), 0))
     rank = jnp.sum(jnp.where(before, 1.0, 0.0), axis=1, keepdims=True)
     slot = rank * NDEV + owners
@@ -328,7 +342,10 @@
     hi, lo = split(zb[...].reshape(PAIRS * QROWS, 256))
     spectrum = dot(jnp.concatenate([hi, lo, hi], 1), b1[...])
     base = jnp.where(la < 2, 0, POLAR) + half * NDEV
-    keep = wave[...] < cut[base + mine]
+    lane_k, q = iota((QROWS, 128), 1), iota((QROWS, 128), 0)
+    k1 = lax.rem(lane_k, 32)
+    live = (q <= 32) & (k1 < K1)
+    keep = live & (jnp.abs(q + 64 * (k1 - 14)) < cut[base + mine])
     spectrum = jnp.where(keep[None], spectrum.reshape(PAIRS, QROWS, 128), 0.0)
     hi, lo = split(spectrum.reshape(PAIRS * QROWS, 128))
     zb[...] = dot(jnp.concatenate([hi, lo, hi], 1), b2[...]).reshape(PAIRS, QROWS, 256)
@@ -365,9 +382,7 @@
         top = x.astype(BF16).astype(F32)
         lb[:, t * 128 : (t + 1) * 128] = jnp.concatenate([top, x - top], 0).astype(BF16)
     places = npl[0].astype(F32)
-    lane_c = iota((NDEV, 128), 1)
-    chosen = jnp.where(lane_c < NDEV, places[:, 0:1], places[:, 1:2])
-    begin = jnp.sum(jnp.where(twice, chosen, 0.0), axis=0, keepdims=True)
+    begin = jnp.concatenate([places[0:1], places[1:2]], 1)
     wide = 256
     point = iota((wide, 128), 0).astype(F32)
 
@@ -425,9 +440,18 @@
 
 def local(model_state, diffusion, coupling, cutoff, strip_list, nest_place):
     vmem = pl.BlockSpec(memory_space=pltpu.VMEM)
-    smem = pl.BlockSpec(memory_space=pltpu.SMEM)
+    hbm = pl.BlockSpec(memory_space=pltpu.HBM)
     dma = pltpu.SemaphoreType.DMA
-    constants = [jnp.asarray(t) for t in tables()]
+    args = [
+        model_state,
+        diffusion,
+        jnp.transpose(coupling, (1, 0, 2)),
+        cutoff,
+        jnp.transpose(strip_list),
+        jnp.transpose(nest_place, (0, 2, 1)),
+        *[jnp.asarray(t) for t in tables()],
+    ]
+    spaces = [pltpu.SMEM if i in (2, 3) else pltpu.VMEM for i in range(len(args))]
     return pl.pallas_call(
         step_kernel,
         name="dynamics_step",
@@ -435,9 +459,11 @@
             jax.ShapeDtypeStruct(model_state.shape, F32),
             jax.ShapeDtypeStruct((1, FIELDS, LEVELS, NB), F32),
         ],
-        in_specs=[vmem, vmem, smem, smem, vmem, vmem] + [vmem] * len(constants),
+        in_specs=[hbm] * len(args),
         out_specs=[vmem, vmem],
         scratch_shapes=[
+            *[space(a.shape, a.dtype) for space, a in zip(spaces, args)],
+            dma((len(args),)),
             pltpu.VMEM((PAIRS, 2, NDEV, 128), F32),
             pltpu.VMEM((PAIRS, NDEV, 128), F32),
             pltpu.VMEM((PAIRS, NDEV, 128), F32),
@@ -462,7 +488,7 @@
         compiler_params=pltpu.CompilerParams(
             collective_id=0, has_side_effects=True, vmem_limit_bytes=48 << 20
         ),
-    )(model_state, diffusion, coupling, cutoff, strip_list, nest_place, *constants)
+    )(*[pltpu.with_memory_space_constraint(a, pltpu.HBM) for a in args])
 
 
 def solution(mesh):

time: 60.4 us -> 49.6 us (0.82)
  local copies, waits for them, and re-layouts: 11.4 us -> 1.67 us
  Pallas kernels: 47.8 us -> 47.1 us
    unnamed x23 -> x2, local copies, waits for them, and re-layouts: 11.4 us -> 1.67 us
    pallas_call x1, Pallas kernels: 47.8 us -> 47.1 us  [local(): pl.pallas_call(step_kernel, name='dynamics_step', out_shape=[jax.ShapeDty...]
where the time goes in v2:
time: 49.6 us; the launch traced here: 49.5 us
  Pallas kernels  47.1 us (95%)
  local copies, waits for them, and re-layouts  1.67 us (3%)
  between operations  0.64 us (1%)
    pallas_call x1, Pallas kernels, local(): pl.pallas_call(step_kernel, name='dynamics_step', out_shape=[jax.ShapeDty...  47.1 us
    unnamed x2, local copies, waits for them, and re-layouts  1.67 us

profile of v2, /device:TPU:1, one launch (start us, length us, event | category | flops | bytes accessed | tf_op | source)
XLA Modules:
  0.0 49.5 jit_solution(9930887392098348325)
XLA Ops:
  0.6 47.1 %dynamics_step.1 = (f32[5,4,56,256]{3,2,1,0:T(8,128)S(1)}, f32[1,5,4,2048]{3,2,1,0:T(4,128)S(1)}) custom-call(f32[5,4,56,256]{3,2,1,0:T(8,128)} %ms_hbm.1, f32[2,256]{1,0:T(2,128)} %dif_hbm.1, f32[5,4,5]{2,1,0:T(4,128)} %bitcast.3, s32[256]{0:T(256)} %cut_hbm.1, s32[4,64]{1,0:T(4,128)} %bitcast.4, s32[1,2,64]{2,1,0:T(2,128)} %bitcast.5, ...), custom_call_target="tpu_custom_call" | custom-call | tf_op jit(solution)/shard_map/dynamics_step/pallas_call | solution.py:455
  47.8 1.0 %copy.15 = f32[5,4,56,256]{3,2,1,0:T(8,128)} copy(f32[5,4,56,256]{3,2,1,0:T(8,128)S(1)} %get-tuple-element.4) | data formatting | bytes 2293760
  48.8 0.7 %copy.16 = f32[1,5,4,2048]{3,2,1,0:T(4,128)} copy(f32[1,5,4,2048]{3,2,1,0:T(4,128)S(1)} %get-tuple-element.5) | data formatting | bytes 327680

commit v3 on v2

--- a/solution.py
+++ b/solution.py
@@ -14,7 +14,7 @@
 PAIRS = FIELDS * LEVELS // 2
 QROWS = 40
 K1 = 28
-CHUNKS = 4
+NZ = 8
 
 
 def hi_lo(table):
@@ -74,8 +74,20 @@
     return jnp.dot(a, b, preferred_element_type=F32)
 
 
-def place_of(device):
-    return lax.rem(device, CHUNKS) * (NDEV // CHUNKS) + lax.div(device, CHUNKS)
+def far_first(step):
+    odd = lax.rem(step, 2) == 1
+    return jnp.where(odd, 4 - lax.div(step + 1, 2), lax.rem(4 + lax.div(step, 2), NZ))
+
+
+def peer(me, k):
+    last = k >= 56
+    side = jnp.where(k < 8, 0, lax.rem(k, 2))
+    ring = jnp.where(k < 8, 0, 2 * lax.div(k - 8, 16) + 1 + side)
+    inner = jnp.where(k < 8, k, lax.div(lax.rem(k - 8, 16), 2))
+    ring = jnp.where(last, NZ - 1, ring)
+    inner = 7 - jnp.where(last, k - 56, inner)
+    z = lax.rem(lax.div(me, NZ) + far_first(ring), NZ)
+    return z * NZ + (lax.rem(me, NZ) ^ inner)
 
 
 def step_kernel(
@@ -93,7 +105,7 @@
     half = jnp.where(is_polar, 0, 1)
     start = pl.multiple_of(jnp.where(la == 3, ROWS - POLAR, 0), 128)
     has_north, has_south = la > 0, la < 3
-    mine = place_of(me)
+    my_z = lax.div(me, NZ)
 
     def remote(src, dst, s, r, lat, lon):
         return pltpu.make_async_remote_copy(
@@ -121,10 +133,10 @@
         greet(la + 1, me)
 
     def greet_plane(k, carry):
-        greet(la, lax.rem(me + k, NDEV))
-        return carry
-
-    lax.fori_loop(1, NDEV, greet_plane, 0)
+        greet(la, peer(me, k))
+        return carry
+
+    lax.fori_loop(0, NDEV - 1, greet_plane, 0)
     for load in loads[: len(early)]:
         load.wait()
 
@@ -172,7 +184,7 @@
             pk[k, 1] = turned[NDEV:]
             return carry
 
-        lax.fori_loop(0, PAIRS, pack, 0)
+        lax.fori_loop(0, PAIRS, pack, 0, unroll=2)
 
     pl.semaphore_wait(barrier, NDEV - 1 + jnp.where(is_polar, 1, 2))
 
@@ -182,15 +194,14 @@
     to_south = remote(ss, hn, s_halo.at[2], r_halo.at[2], jnp.minimum(la + 1, 3), me)
     to_north = remote(sn, hs, s_halo.at[3], r_halo.at[3], jnp.maximum(la - 1, 0), me)
 
-    size = NDEV // CHUNKS
 
     def relay(g):
-        rows = pl.ds(g * size, size)
+        rows = pl.ds(lax.rem(my_z + far_first(g), NZ) * NZ, NZ)
         return remote(pk.at[:, 1, rows], rl.at[:, rows], s_rel.at[g], r_rel.at[g], helper_lat, me)
 
     @pl.when(is_polar)
     def _():
-        for g in range(CHUNKS):
+        for g in range(NZ):
             relay(g).start()
 
     to_east.start()
@@ -200,32 +211,28 @@
 
     @pl.when(is_polar)
     def _():
-        pltpu.make_async_copy(pk.at[:, 0, mine], arr.at[:, me], r_fwd).start()
+        pltpu.make_async_copy(pk.at[:, 0, me], arr.at[:, me], r_fwd).start()
 
         def send(k, carry):
-            d = lax.rem(me + k, NDEV)
-            remote(pk.at[:, 0, place_of(d)], arr.at[:, me], s_fwd, r_fwd, la, d).start()
+            d = peer(me, k)
+            remote(pk.at[:, 0, d], arr.at[:, me], s_fwd, r_fwd, la, d).start()
             return carry
 
-        lax.fori_loop(1, NDEV, send, 0)
+        lax.fori_loop(0, NDEV - 1, send, 0)
 
     @pl.when(is_helper)
     def _():
-        for g in range(CHUNKS):
+        for g in range(NZ):
             relay(g).wait_recv()
 
             def send(i, carry, g=g):
-                b = lax.rem(i + lax.div(me, CHUNKS), size)
-                d = b * CHUNKS + g
-
-                @pl.when(d != me)
-                def _():
-                    remote(rl.at[:, g * size + b], arr.at[:, me], s_fwd, r_fwd, la, d).start()
-
+                z = lax.rem(my_z + far_first(g), NZ)
+                d = z * NZ + (lax.rem(me, NZ) ^ (7 - i))
+                remote(rl.at[:, d], arr.at[:, me], s_fwd, r_fwd, la, d).start()
                 return carry
 
-            lax.fori_loop(0, size, send, 0)
-        pltpu.make_async_copy(rl.at[:, mine], arr.at[:, me], r_fwd).start()
+            lax.fori_loop(0, NZ - (g == NZ - 1), send, 0)
+        pltpu.make_async_copy(rl.at[:, me], arr.at[:, me], r_fwd).start()
 
     for load in loads[len(early) :]:
         load.wait()
@@ -249,7 +256,7 @@
             out[f, l, :, 0:128] += jnp.where(lane_u == 0, d * value, 0.0)
             return carry
 
-        lax.fori_loop(0, FIELDS * LEVELS, fix, 0)
+        lax.fori_loop(0, FIELDS * LEVELS, fix, 0, unroll=4)
 
     @pl.when(has_south)
     def _():
@@ -263,7 +270,7 @@
             out[f, l, :, 128:256] += jnp.where(lane_u == 127, d * value, 0.0)
             return carry
 
-        lax.fori_loop(0, FIELDS * LEVELS, fix, 0)
+        lax.fori_loop(0, FIELDS * LEVELS, fix, 0, unroll=4)
 
     eye = iota((NDEV, NDEV), 0) == iota((NDEV, NDEV), 1)
 
@@ -298,7 +305,7 @@
         xs[u] = a
         return carry
 
-    lax.fori_loop(0, FIELDS * LEVELS, strips_of, 0)
+    lax.fori_loop(0, FIELDS * LEVELS, strips_of, 0, unroll=4)
     window = lax.div(lane, 32)
     for g in range(3):
         both = []
@@ -321,11 +328,11 @@
     pltpu.make_async_copy(sb.at[:, :, me], rb.at[:, :, me], r_nest).start()
 
     def send_strips(k, carry):
-        d = lax.rem(me + k, NDEV)
+        d = peer(me, k)
         remote(sb.at[:, :, d], rb.at[:, :, me], s_nest, r_nest, la, d).start()
         return carry
 
-    lax.fori_loop(1, NDEV, send_strips, 0)
+    lax.fori_loop(0, NDEV - 1, send_strips, 0)
 
     pltpu.make_async_copy(arr, arr, r_fwd).wait()
     cos, sin = tw[0], tw[1]
@@ -338,14 +345,14 @@
         zb[k, :, 128:256] = im * cos - re * sin
         return carry
 
-    lax.fori_loop(0, PAIRS, forward, 0)
+    lax.fori_loop(0, PAIRS, forward, 0, unroll=True)
     hi, lo = split(zb[...].reshape(PAIRS * QROWS, 256))
     spectrum = dot(jnp.concatenate([hi, lo, hi], 1), b1[...])
     base = jnp.where(la < 2, 0, POLAR) + half * NDEV
     lane_k, q = iota((QROWS, 128), 1), iota((QROWS, 128), 0)
     k1 = lax.rem(lane_k, 32)
     live = (q <= 32) & (k1 < K1)
-    keep = live & (jnp.abs(q + 64 * (k1 - 14)) < cut[base + mine])
+    keep = live & (jnp.abs(q + 64 * (k1 - 14)) < cut[base + me])
     spectrum = jnp.where(keep[None], spectrum.reshape(PAIRS, QROWS, 128), 0.0)
     hi, lo = split(spectrum.reshape(PAIRS * QROWS, 128))
     zb[...] = dot(jnp.concatenate([hi, lo, hi], 1), b2[...]).reshape(PAIRS, QROWS, 256)
@@ -357,22 +364,22 @@
         res[k] = dot(c2[...], jnp.concatenate([hi, lo, hi], 0))
         return carry
 
-    lax.fori_loop(0, PAIRS, backward, 0)
+    lax.fori_loop(0, PAIRS, backward, 0, unroll=True)
 
     @pl.when(is_polar)
     def _():
-        pltpu.make_async_copy(res.at[:, me], ret.at[:, 0, mine], r_ret).start()
+        pltpu.make_async_copy(res.at[:, me], ret.at[:, 0, me], r_ret).start()
 
     @pl.when(is_helper)
     def _():
-        remote(res.at[:, me], ret.at[:, 1, mine], s_ret, r_ret, polar_lat, me).start()
+        remote(res.at[:, me], ret.at[:, 1, me], s_ret, r_ret, polar_lat, me).start()
 
     def send_back(k, carry):
-        d = lax.rem(me + k, NDEV)
-        remote(res.at[:, d], ret.at[:, half, mine], s_ret, r_ret, polar_lat, d).start()
-        return carry
-
-    lax.fori_loop(1, NDEV, send_back, 0)
+        d = peer(me, k)
+        remote(res.at[:, d], ret.at[:, half, me], s_ret, r_ret, polar_lat, d).start()
+        return carry
+
+    lax.fori_loop(0, NDEV - 1, send_back, 0)
 
     pltpu.make_async_copy(rb, rb, r_nest).wait()
     for g in range(3):
@@ -404,7 +411,7 @@
             nest[0, f, :, pl.ds(first, wide)] = total[f * LEVELS : (f + 1) * LEVELS]
         return carry
 
-    lax.fori_loop(0, NB // wide, boundary, 0)
+    lax.fori_loop(0, NB // wide, boundary, 0, unroll=2)
 
     @pl.when(is_polar)
     def _():
@@ -417,7 +424,7 @@
             out[f, l0 + 1, :, pl.ds(start, POLAR)] = turned[64 : 64 + COLS]
             return carry
 
-        lax.fori_loop(0, PAIRS, unpack, 0)
+        lax.fori_loop(0, PAIRS, unpack, 0, unroll=5)
 
     to_east.wait_send()
     to_west.wait_send()
@@ -429,7 +436,7 @@
 
     @pl.when(is_polar)
     def _():
-        for g in range(CHUNKS):
+        for g in range(NZ):
             relay(g).wait_send()
         pltpu.make_async_copy(res.at[:, others], res.at[:, others], s_ret).wait()
 
@@ -481,7 +488,7 @@
             pltpu.VMEM((3, 2, NDEV, 128), F32),
             pltpu.VMEM((3, 128, 128), F32),
             pltpu.VMEM((48, STRIP * 128), BF16),
-            dma((CHUNKS,)), dma((CHUNKS,)),
+            dma((NZ,)), dma((NZ,)),
             dma, dma, dma, dma, dma, dma,
             dma((4,)), dma((4,)),
         ],

time: 49.6 us -> 42.1 us (0.85)
  Pallas kernels: 47.1 us -> 39.8 us
    pallas_call x1, Pallas kernels: 47.1 us -> 39.8 us  [local(): pl.pallas_call(step_kernel, name='dynamics_step', out_shape=[jax.ShapeDty...]
where the time goes in v3:
time: 42.1 us
  Pallas kernels  39.8 us (95%)
  local copies, waits for them, and re-layouts  1.67 us (4%)
  between operations  0.64 us (2%)
    pallas_call x1, Pallas kernels, local(): pl.pallas_call(step_kernel, name='dynamics_step', out_shape=[jax.ShapeDty...  39.8 us
    unnamed x2, local copies, waits for them, and re-layouts  1.67 us

profile of v3, /device:TPU:1, one launch (start us, length us, event | category | flops | bytes accessed | tf_op | source)
XLA Modules:
  0.0 42.1 jit_solution(11778773010533776713)
XLA Ops:
  0.6 39.8 %dynamics_step.1 = (f32[5,4,56,256]{3,2,1,0:T(8,128)S(1)}, f32[1,5,4,2048]{3,2,1,0:T(4,128)S(1)}) custom-call(f32[5,4,56,256]{3,2,1,0:T(8,128)} %ms_hbm.1, f32[2,256]{1,0:T(2,128)} %dif_hbm.1, f32[5,4,5]{2,1,0:T(4,128)} %bitcast.3, s32[256]{0:T(256)} %cut_hbm.1, s32[4,64]{1,0:T(4,128)} %bitcast.4, s32[1,2,64]{2,1,0:T(2,128)} %bitcast.5, ...), custom_call_target="tpu_custom_call" | custom-call | tf_op jit(solution)/shard_map/dynamics_step/pallas_call | solution.py:462
  40.4 1.0 %copy.15 = f32[5,4,56,256]{3,2,1,0:T(8,128)} copy(f32[5,4,56,256]{3,2,1,0:T(8,128)S(1)} %get-tuple-element.4) | data formatting | bytes 2293760
  41.4 0.7 %copy.16 = f32[1,5,4,2048]{3,2,1,0:T(4,128)} copy(f32[1,5,4,2048]{3,2,1,0:T(4,128)S(1)} %get-tuple-element.5) | data formatting | bytes 327680

commit v4 on v3

--- a/solution.py
+++ b/solution.py
@@ -92,9 +92,9 @@
 
 def step_kernel(
     ms_hbm, dif_hbm, coup_hbm, cut_hbm, sl_hbm, npl_hbm, c1_hbm, tw_hbm, b1_hbm, b2_hbm, c2_hbm,
-    out, nest,
+    out, nest, ret,
     ms, dif, coup, cut, sl, npl, c1, tw, b1, b2, c2, s_load,
-    pk, rl, arr, res, ret, zb, sn, ss, hw, he, hn, hs, xs, sb, rb, tb, lb,
+    pk, rl, arr, res, zb, sn, ss, hw, he, hn, hs, xs, sb, rb, tb, lb,
     s_rel, r_rel, s_fwd, r_fwd, s_ret, r_ret, s_nest, r_nest, s_halo, r_halo,
 ):
     la, me = lax.axis_index("lat"), lax.axis_index("lon")
@@ -199,11 +199,6 @@
         rows = pl.ds(lax.rem(my_z + far_first(g), NZ) * NZ, NZ)
         return remote(pk.at[:, 1, rows], rl.at[:, rows], s_rel.at[g], r_rel.at[g], helper_lat, me)
 
-    @pl.when(is_polar)
-    def _():
-        for g in range(NZ):
-            relay(g).start()
-
     to_east.start()
     to_west.start()
     pl.when(has_south)(to_south.start)
@@ -211,6 +206,11 @@
 
     @pl.when(is_polar)
     def _():
+        for g in range(NZ):
+            relay(g).start()
+
+    @pl.when(is_polar)
+    def _():
         pltpu.make_async_copy(pk.at[:, 0, me], arr.at[:, me], r_fwd).start()
 
         def send(k, carry):
@@ -220,57 +220,8 @@
 
         lax.fori_loop(0, NDEV - 1, send, 0)
 
-    @pl.when(is_helper)
-    def _():
-        for g in range(NZ):
-            relay(g).wait_recv()
-
-            def send(i, carry, g=g):
-                z = lax.rem(my_z + far_first(g), NZ)
-                d = z * NZ + (lax.rem(me, NZ) ^ (7 - i))
-                remote(rl.at[:, d], arr.at[:, me], s_fwd, r_fwd, la, d).start()
-                return carry
-
-            lax.fori_loop(0, NZ - (g == NZ - 1), send, 0)
-        pltpu.make_async_copy(rl.at[:, me], arr.at[:, me], r_fwd).start()
-
     for load in loads[len(early) :]:
         load.wait()
-
-    to_east.wait_recv()
-    to_west.wait_recv()
-    for f in range(FIELDS):
-        for l in range(LEVELS):
-            out[f, l, 0:1] += d0 * hw[f, l]
-            out[f, l, COLS - 1 : COLS] += d0 * he[f, l]
-
-    @pl.when(has_north)
-    def _():
-        to_south.wait_recv()
-        halo = hn[...]
-        d = dif[1:2, 0:128]
-
-        def fix(u, carry):
-            f, l = lax.div(u, LEVELS), lax.rem(u, LEVELS)
-            value = pltpu.roll(halo, lax.rem(128 - u, 128), 1)
-            out[f, l, :, 0:128] += jnp.where(lane_u == 0, d * value, 0.0)
-            return carry
-
-        lax.fori_loop(0, FIELDS * LEVELS, fix, 0, unroll=4)
-
-    @pl.when(has_south)
-    def _():
-        to_north.wait_recv()
-        halo = hs[...]
-        d = dif[1:2, 128:256]
-
-        def fix(u, carry):
-            f, l = lax.div(u, LEVELS), lax.rem(u, LEVELS)
-            value = pltpu.roll(halo, 127 - u, 1)
-            out[f, l, :, 128:256] += jnp.where(lane_u == 127, d * value, 0.0)
-            return carry
-
-        lax.fori_loop(0, FIELDS * LEVELS, fix, 0, unroll=4)
 
     eye = iota((NDEV, NDEV), 0) == iota((NDEV, NDEV), 1)
 
@@ -287,12 +238,47 @@
     slot_row = jnp.sum(jnp.where(twice, slot, 0.0), axis=0, keepdims=True)
     routing = jnp.where(iota((128, 128), 0).astype(F32) == slot_row, 1.0, 0.0).astype(BF16)
     pick = jnp.where(lax.rem(iota((NDEV, 128), 1), NDEV) == columns, 1.0, 0.0).astype(BF16)
-    high = offsets >= 128
+    lane = iota((NDEV, 128), 1)
+    high = jnp.broadcast_to(offsets, (NDEV, 128)) >= 128
     inner = lax.rem(offsets, 128)
-    lane = iota((NDEV, 128), 1)
     spill = (lane < STRIP) & (inner > 128 - STRIP)
-    bits = lax.div(inner, 1)
+    bits = jnp.broadcast_to(inner, (NDEV, 128))
     zero8 = jnp.zeros((8, ROWS), F32)
+
+    to_east.wait_recv()
+    to_west.wait_recv()
+    for f in range(FIELDS):
+        for l in range(LEVELS):
+            out[f, l, 0:1] += d0 * hw[f, l]
+            out[f, l, COLS - 1 : COLS] += d0 * he[f, l]
+
+    @pl.when(has_north)
+    def _():
+        to_south.wait_recv()
+        halo = hn[...]
+        d = dif[1:2, 0:128]
+
+        def fix(u, carry):
+            f, l = lax.div(u, LEVELS), lax.rem(u, LEVELS)
+            value = pltpu.roll(halo, lax.rem(128 - u, 128), 1)
+            out[f, l, :, 0:128] += jnp.where(lane_u == 0, d * value, 0.0)
+            return carry
+
+        lax.fori_loop(0, FIELDS * LEVELS, fix, 0, unroll=4)
+
+    @pl.when(has_south)
+    def _():
+        to_north.wait_recv()
+        halo = hs[...]
+        d = dif[1:2, 128:256]
+
+        def fix(u, carry):
+            f, l = lax.div(u, LEVELS), lax.rem(u, LEVELS)
+            value = pltpu.roll(halo, 127 - u, 1)
+            out[f, l, :, 128:256] += jnp.where(lane_u == 127, d * value, 0.0)
+            return carry
+
+        lax.fori_loop(0, FIELDS * LEVELS, fix, 0, unroll=4)
 
     def strips_of(u, carry):
         x = out[lax.div(u, LEVELS), lax.rem(u, LEVELS)]
@@ -305,7 +291,22 @@
         xs[u] = a
         return carry
 
+    @pl.when(is_helper)
+    def _():
+        for g in range(NZ):
+            relay(g).wait_recv()
+
+            def send(i, carry, g=g):
+                z = lax.rem(my_z + far_first(g), NZ)
+                d = z * NZ + (lax.rem(me, NZ) ^ (7 - i))
+                remote(rl.at[:, d], arr.at[:, me], s_fwd, r_fwd, la, d).start()
+                return carry
+
+            lax.fori_loop(0, NZ - (g == NZ - 1), send, 0)
+        pltpu.make_async_copy(rl.at[:, me], arr.at[:, me], r_fwd).start()
+
     lax.fori_loop(0, FIELDS * LEVELS, strips_of, 0, unroll=4)
+
     window = lax.div(lane, 32)
     for g in range(3):
         both = []
@@ -325,14 +326,17 @@
         sb[g, 0] = a[:NDEV]
         sb[g, 1] = a[NDEV:]
 
-    pltpu.make_async_copy(sb.at[:, :, me], rb.at[:, :, me], r_nest).start()
-
-    def send_strips(k, carry):
-        d = peer(me, k)
-        remote(sb.at[:, :, d], rb.at[:, :, me], s_nest, r_nest, la, d).start()
-        return carry
-
-    lax.fori_loop(0, NDEV - 1, send_strips, 0)
+    def send_nest():
+        pltpu.make_async_copy(sb.at[:, :, me], rb.at[:, :, me], r_nest).start()
+
+        def send(k, carry):
+            d = peer(me, k)
+            remote(sb.at[:, :, d], rb.at[:, :, me], s_nest, r_nest, la, d).start()
+            return carry
+
+        lax.fori_loop(0, NDEV - 1, send, 0)
+
+    send_nest()
 
     pltpu.make_async_copy(arr, arr, r_fwd).wait()
     cos, sin = tw[0], tw[1]
@@ -395,14 +399,14 @@
 
     def boundary(n, carry):
         first = pl.multiple_of(n * wide, wide)
-        away = point + (n * wide).astype(F32) - begin
+        away = jnp.clip(point + (n * wide).astype(F32) - begin, -32.0, 224.0).astype(BF16)
         hats = []
         for t in range(STRIP):
             d = away - float(RATIO * t)
             hat = jnp.maximum(float(RATIO) - jnp.abs(d), 0.0)
             if t == 0:
-                hat = jnp.where(d >= 0.0, hat, 0.0)
-            hats.append(hat.astype(BF16))
+                hat = jnp.where(d >= 0.0, hat, jnp.zeros_like(hat))
+            hats.append(hat)
         total = lax.dot_general(
             lb[...], jnp.concatenate(hats, 1), (((1,), (1,)), ((), ())), preferred_element_type=F32
         )
@@ -416,15 +420,6 @@
     @pl.when(is_polar)
     def _():
         pltpu.make_async_copy(ret, ret, r_ret).wait()
-
-        def unpack(k, carry):
-            f, l0 = lax.div(k, 2), 2 * lax.rem(k, 2)
-            turned = jnp.concatenate([ret[k, 0], ret[k, 1]], 0).T
-            out[f, l0, :, pl.ds(start, POLAR)] = turned[:COLS]
-            out[f, l0 + 1, :, pl.ds(start, POLAR)] = turned[64 : 64 + COLS]
-            return carry
-
-        lax.fori_loop(0, PAIRS, unpack, 0, unroll=5)
 
     to_east.wait_send()
     to_west.wait_send()
@@ -443,6 +438,45 @@
     @pl.when(is_helper)
     def _():
         pltpu.make_async_copy(res, res, s_ret).wait()
+
+
+def place_kernel(upd, nest, ret, out, nest_out, rows, sem):
+    la = lax.axis_index("lat")
+    is_polar = (la == 0) | (la == 3)
+    start = pl.multiple_of(jnp.where(la == 3, ROWS - POLAR, 0), 128)
+    other = pl.multiple_of(ROWS - POLAR - start, 128)
+    nest_copy = pltpu.make_async_copy(nest, nest_out, sem.at[0])
+    nest_copy.start()
+
+    @pl.when(is_polar)
+    def _():
+        rest = (slice(None),) * 3 + (pl.ds(other, ROWS - POLAR),)
+        rest_copy = pltpu.make_async_copy(upd.at[rest], out.at[rest], sem.at[1])
+        rest_copy.start()
+        copies = []
+        for k in range(PAIRS):
+            f, l0 = k // 2, 2 * (k % 2)
+            turned = jnp.concatenate([ret[k, 0], ret[k, 1]], 0).T
+            rows[f, l0] = turned[:COLS]
+            rows[f, l0 + 1] = turned[64 : 64 + COLS]
+            pair = pl.ds(l0, 2)
+            copies.append(
+                pltpu.make_async_copy(
+                    rows.at[f, pair], out.at[f, pair, :, pl.ds(start, POLAR)], sem.at[2 + k]
+                )
+            )
+            copies[k].start()
+        rest_copy.wait()
+        for copy in copies:
+            copy.wait()
+
+    @pl.when(jnp.logical_not(is_polar))
+    def _():
+        whole = pltpu.make_async_copy(upd, out, sem.at[1])
+        whole.start()
+        whole.wait()
+
+    nest_copy.wait()
 
 
 def local(model_state, diffusion, coupling, cutoff, strip_list, nest_place):
@@ -459,15 +493,16 @@
         *[jnp.asarray(t) for t in tables()],
     ]
     spaces = [pltpu.SMEM if i in (2, 3) else pltpu.VMEM for i in range(len(args))]
-    return pl.pallas_call(
+    updated, nest, filtered = pl.pallas_call(
         step_kernel,
         name="dynamics_step",
         out_shape=[
             jax.ShapeDtypeStruct(model_state.shape, F32),
             jax.ShapeDtypeStruct((1, FIELDS, LEVELS, NB), F32),
+            jax.ShapeDtypeStruct((PAIRS, 2, NDEV, 128), F32),
         ],
         in_specs=[hbm] * len(args),
-        out_specs=[vmem, vmem],
+        out_specs=[vmem, vmem, vmem],
         scratch_shapes=[
             *[space(a.shape, a.dtype) for space, a in zip(spaces, args)],
             dma((len(args),)),
@@ -475,7 +510,6 @@
             pltpu.VMEM((PAIRS, NDEV, 128), F32),
             pltpu.VMEM((PAIRS, NDEV, 128), F32),
             pltpu.VMEM((PAIRS, NDEV, 128), F32),
-            pltpu.VMEM((PAIRS, 2, NDEV, 128), F32),
             pltpu.VMEM((PAIRS, QROWS, 256), F32),
             pltpu.VMEM((COLS, 128), F32),
             pltpu.VMEM((COLS, 128), F32),
@@ -496,6 +530,18 @@
             collective_id=0, has_side_effects=True, vmem_limit_bytes=48 << 20
         ),
     )(*[pltpu.with_memory_space_constraint(a, pltpu.HBM) for a in args])
+    return pl.pallas_call(
+        place_kernel,
+        name="place_filtered",
+        out_shape=[
+            jax.ShapeDtypeStruct(updated.shape, F32),
+            jax.ShapeDtypeStruct(nest.shape, F32),
+        ],
+        in_specs=[vmem, vmem, vmem],
+        out_specs=[hbm, hbm],
+        scratch_shapes=[pltpu.VMEM((FIELDS, LEVELS, COLS, POLAR), F32), dma((2 + PAIRS,))],
+        compiler_params=pltpu.CompilerParams(vmem_limit_bytes=16 << 20),
+    )(updated, nest, filtered)
 
 
 def solution(mesh):

time: 42.1 us -> 40.6 us (0.964)
  local copies, waits for them, and re-layouts: 1.67 us -> 0 us
    unnamed x2 -> x0, local copies, waits for them, and re-layouts: 1.67 us -> none
    pallas_call x0 -> x1, Pallas kernels: none -> 1.14 us  [local(): pl.pallas_call(place_kernel, name='place_filtered', out_shape=[jax.ShapeD...]
    pallas_call x1, Pallas kernels: 39.8 us -> 38.7 us  [local(): pl.pallas_call(step_kernel, name='dynamics_step', out_shape=[jax.ShapeDty...]
where the time goes in v4:
time: 40.6 us; the launch traced here: 40.5 us
  Pallas kernels  39.8 us (98%)
  between operations  0.64 us (2%)
    pallas_call x1, Pallas kernels, local(): pl.pallas_call(step_kernel, name='dynamics_step', out_shape=[jax.ShapeDty...  38.7 us
    pallas_call x1, Pallas kernels, local(): pl.pallas_call(place_kernel, name='place_filtered', out_shape=[jax.ShapeD...  1.14 us

profile of v4, /device:TPU:1, one launch (start us, length us, event | category | flops | bytes accessed | tf_op | source)
XLA Modules:
  0.0 40.5 jit_solution(1377480231203779791)
XLA Ops:
  0.6 38.7 %dynamics_step.1 = (f32[5,4,56,256]{3,2,1,0:T(8,128)S(1)}, f32[1,5,4,2048]{3,2,1,0:T(4,128)S(1)}, f32[10,2,64,128]{3,2,1,0:T(8,128)S(1)}) custom-call(f32[5,4,56,256]{3,2,1,0:T(8,128)} %ms_hbm.1, f32[2,256]{1,0:T(2,128)} %dif_hbm.1, f32[5,4,5]{2,1,0:T(4,128)} %bitcast.3, s32[256]{0:T(256)} %cut_hbm.1, s32[4,64]{1,0:T(4,128)} %bitcast.4, ...), custom_call_target="tpu_custom_call" | custom-call | tf_op jit(solution)/shard_map/dynamics_step/pallas_call | solution.py:496
  39.3 1.1 %place_filtered.1 = (f32[5,4,56,256]{3,2,1,0:T(8,128)}, f32[1,5,4,2048]{3,2,1,0:T(4,128)}) custom-call(f32[5,4,56,256]{3,2,1,0:T(8,128)S(1)} %get-tuple-element.5.upd, f32[1,5,4,2048]{3,2,1,0:T(4,128)S(1)} %get-tuple-element.6.nest, f32[10,2,64,128]{3,2,1,0:T(8,128)S(1)} %get-tuple-element.7.ret), custom_call_target="tpu_custom_call" | custom-call | tf_op jit(solution)/shard_map/place_filtered/pallas_call | solution.py:533

commit v5 on v4

--- a/solution.py
+++ b/solution.py
@@ -245,40 +245,32 @@
     bits = jnp.broadcast_to(inner, (NDEV, 128))
     zero8 = jnp.zeros((8, ROWS), F32)
 
-    to_east.wait_recv()
-    to_west.wait_recv()
-    for f in range(FIELDS):
-        for l in range(LEVELS):
-            out[f, l, 0:1] += d0 * hw[f, l]
-            out[f, l, COLS - 1 : COLS] += d0 * he[f, l]
-
-    @pl.when(has_north)
-    def _():
-        to_south.wait_recv()
-        halo = hn[...]
-        d = dif[1:2, 0:128]
+    def fix_lon():
+        to_east.wait_recv()
+        to_west.wait_recv()
+        for f in range(FIELDS):
+            for l in range(LEVELS):
+                out[f, l, 0:1] += d0 * hw[f, l]
+                out[f, l, COLS - 1 : COLS] += d0 * he[f, l]
+
+    def fix_lat(copy, buffer, tile, row):
+        copy.wait_recv()
+        halo = buffer[...]
+        d = dif[1:2, tile : tile + 128]
 
         def fix(u, carry):
             f, l = lax.div(u, LEVELS), lax.rem(u, LEVELS)
-            value = pltpu.roll(halo, lax.rem(128 - u, 128), 1)
-            out[f, l, :, 0:128] += jnp.where(lane_u == 0, d * value, 0.0)
+            value = pltpu.roll(halo, lax.rem(128 + row - u, 128), 1)
+            out[f, l, :, tile : tile + 128] += jnp.where(lane_u == row, d * value, 0.0)
             return carry
 
         lax.fori_loop(0, FIELDS * LEVELS, fix, 0, unroll=4)
 
-    @pl.when(has_south)
-    def _():
-        to_north.wait_recv()
-        halo = hs[...]
-        d = dif[1:2, 128:256]
-
-        def fix(u, carry):
-            f, l = lax.div(u, LEVELS), lax.rem(u, LEVELS)
-            value = pltpu.roll(halo, 127 - u, 1)
-            out[f, l, :, 128:256] += jnp.where(lane_u == 127, d * value, 0.0)
-            return carry
-
-        lax.fori_loop(0, FIELDS * LEVELS, fix, 0, unroll=4)
+    def fix_north():
+        fix_lat(to_south, hn, 0, 0)
+
+    def fix_south():
+        fix_lat(to_north, hs, 128, 127)
 
     def strips_of(u, carry):
         x = out[lax.div(u, LEVELS), lax.rem(u, LEVELS)]
@@ -291,8 +283,15 @@
         xs[u] = a
         return carry
 
+    def cut_strips(first, last):
+        lax.fori_loop(first, last, strips_of, 0, unroll=4)
+
     @pl.when(is_helper)
     def _():
+        between = {
+            0: fix_lon, 1: fix_north, 2: fix_south,
+            3: lambda: cut_strips(0, 4), 4: lambda: cut_strips(4, 8), 5: lambda: cut_strips(8, 12), 6: lambda: cut_strips(12, 16)
+        }
         for g in range(NZ):
             relay(g).wait_recv()
 
@@ -303,9 +302,17 @@
                 return carry
 
             lax.fori_loop(0, NZ - (g == NZ - 1), send, 0)
+            if g in between:
+                between[g]()
         pltpu.make_async_copy(rl.at[:, me], arr.at[:, me], r_fwd).start()
-
-    lax.fori_loop(0, FIELDS * LEVELS, strips_of, 0, unroll=4)
+        cut_strips(16, FIELDS * LEVELS)
+
+    @pl.when(is_polar)
+    def _():
+        fix_lon()
+        pl.when(has_north)(fix_north)
+        pl.when(has_south)(fix_south)
+        cut_strips(0, FIELDS * LEVELS)
 
     window = lax.div(lane, 32)
     for g in range(3):

time: 40.6 us -> 39.5 us (0.973)
  Pallas kernels: 39.8 us -> 38.8 us
    pallas_call x1, Pallas kernels: 38.7 us -> 37.6 us  [local(): pl.pallas_call(step_kernel, name='dynamics_step', out_shape=[jax.ShapeDty...]
where the time goes in v5:
time: 39.5 us; the launch traced here: 39.4 us
  Pallas kernels  38.8 us (98%)
  between operations  0.64 us (2%)
    pallas_call x1, Pallas kernels, local(): pl.pallas_call(step_kernel, name='dynamics_step', out_shape=[jax.ShapeDty...  37.6 us
    pallas_call x1, Pallas kernels, local(): pl.pallas_call(place_kernel, name='place_filtered', out_shape=[jax.ShapeD...  1.14 us

profile of v5, /device:TPU:1, one launch (start us, length us, event | category | flops | bytes accessed | tf_op | source)
XLA Modules:
  0.0 39.4 jit_solution(14498557838797729701)
XLA Ops:
  0.6 37.6 %dynamics_step.1 = (f32[5,4,56,256]{3,2,1,0:T(8,128)S(1)}, f32[1,5,4,2048]{3,2,1,0:T(4,128)S(1)}, f32[10,2,64,128]{3,2,1,0:T(8,128)S(1)}) custom-call(f32[5,4,56,256]{3,2,1,0:T(8,128)} %ms_hbm.1, f32[2,256]{1,0:T(2,128)} %dif_hbm.1, f32[5,4,5]{2,1,0:T(4,128)} %bitcast.3, s32[256]{0:T(256)} %cut_hbm.1, s32[4,64]{1,0:T(4,128)} %bitcast.4, ...), custom_call_target="tpu_custom_call" | custom-call | tf_op jit(solution)/shard_map/dynamics_step/pallas_call | solution.py:503
  38.3 1.1 %place_filtered.1 = (f32[5,4,56,256]{3,2,1,0:T(8,128)}, f32[1,5,4,2048]{3,2,1,0:T(4,128)}) custom-call(f32[5,4,56,256]{3,2,1,0:T(8,128)S(1)} %get-tuple-element.5.upd, f32[1,5,4,2048]{3,2,1,0:T(4,128)S(1)} %get-tuple-element.6.nest, f32[10,2,64,128]{3,2,1,0:T(8,128)S(1)} %get-tuple-element.7.ret), custom_call_target="tpu_custom_call" | custom-call | tf_op jit(solution)/shard_map/place_filtered/pallas_call | solution.py:540

commit v6 on v5

--- a/solution.py
+++ b/solution.py
@@ -12,6 +12,8 @@
 FIELDS, LEVELS, COLS, ROWS = 5, 4, 56, 256
 NLON, NDEV, POLAR, NB, RATIO, STRIP = 3584, 64, 128, 2048, 11, 16
 PAIRS = FIELDS * LEVELS // 2
+PARTS = 2
+SIZE = PAIRS // PARTS
 QROWS = 40
 K1 = 28
 NZ = 8
@@ -195,9 +197,12 @@
     to_north = remote(sn, hs, s_halo.at[3], r_halo.at[3], jnp.maximum(la - 1, 0), me)
 
 
-    def relay(g):
+    def relay(part, g):
         rows = pl.ds(lax.rem(my_z + far_first(g), NZ) * NZ, NZ)
-        return remote(pk.at[:, 1, rows], rl.at[:, rows], s_rel.at[g], r_rel.at[g], helper_lat, me)
+        pairs, i = pl.ds(part * SIZE, SIZE), part * NZ + g
+        return remote(
+            pk.at[pairs, 1, rows], rl.at[pairs, rows], s_rel.at[i], r_rel.at[i], helper_lat, me
+        )
 
     to_east.start()
     to_west.start()
@@ -206,19 +211,22 @@
 
     @pl.when(is_polar)
     def _():
-        for g in range(NZ):
-            relay(g).start()
-
-    @pl.when(is_polar)
-    def _():
-        pltpu.make_async_copy(pk.at[:, 0, me], arr.at[:, me], r_fwd).start()
-
-        def send(k, carry):
-            d = peer(me, k)
-            remote(pk.at[:, 0, d], arr.at[:, me], s_fwd, r_fwd, la, d).start()
-            return carry
-
-        lax.fori_loop(0, NDEV - 1, send, 0)
+        for part in range(PARTS):
+            for g in range(NZ):
+                relay(part, g).start()
+
+    @pl.when(is_polar)
+    def _():
+        for part in range(PARTS):
+            pairs, s, r = pl.ds(part * SIZE, SIZE), s_fwd.at[part], r_fwd.at[part]
+            pltpu.make_async_copy(pk.at[pairs, 0, me], arr.at[pairs, me], r).start()
+
+            def send(k, carry, pairs=pairs, s=s, r=r):
+                d = peer(me, k)
+                remote(pk.at[pairs, 0, d], arr.at[pairs, me], s, r, la, d).start()
+                return carry
+
+            lax.fori_loop(0, NDEV - 1, send, 0)
 
     for load in loads[len(early) :]:
         load.wait()
@@ -289,23 +297,25 @@
     @pl.when(is_helper)
     def _():
         between = {
-            0: fix_lon, 1: fix_north, 2: fix_south,
-            3: lambda: cut_strips(0, 4), 4: lambda: cut_strips(4, 8), 5: lambda: cut_strips(8, 12), 6: lambda: cut_strips(12, 16)
+            7: fix_lon, 8: fix_north, 9: fix_south,
+            11: lambda: cut_strips(0, 4), 12: lambda: cut_strips(4, 8), 13: lambda: cut_strips(8, 12)
         }
-        for g in range(NZ):
-            relay(g).wait_recv()
-
-            def send(i, carry, g=g):
-                z = lax.rem(my_z + far_first(g), NZ)
-                d = z * NZ + (lax.rem(me, NZ) ^ (7 - i))
-                remote(rl.at[:, d], arr.at[:, me], s_fwd, r_fwd, la, d).start()
-                return carry
-
-            lax.fori_loop(0, NZ - (g == NZ - 1), send, 0)
-            if g in between:
-                between[g]()
-        pltpu.make_async_copy(rl.at[:, me], arr.at[:, me], r_fwd).start()
-        cut_strips(16, FIELDS * LEVELS)
+        for part in range(PARTS):
+            pairs, s, r = pl.ds(part * SIZE, SIZE), s_fwd.at[part], r_fwd.at[part]
+            for g in range(NZ):
+                relay(part, g).wait_recv()
+
+                def send(i, carry, g=g, pairs=pairs, s=s, r=r):
+                    z = lax.rem(my_z + far_first(g), NZ)
+                    d = z * NZ + (lax.rem(me, NZ) ^ (7 - i))
+                    remote(rl.at[pairs, d], arr.at[pairs, me], s, r, la, d).start()
+                    return carry
+
+                lax.fori_loop(0, NZ - (g == NZ - 1), send, 0)
+                if part * NZ + g in between:
+                    between[part * NZ + g]()
+            pltpu.make_async_copy(rl.at[pairs, me], arr.at[pairs, me], r).start()
+        cut_strips(12, FIELDS * LEVELS)
 
     @pl.when(is_polar)
     def _():
@@ -345,52 +355,58 @@
 
     send_nest()
 
-    pltpu.make_async_copy(arr, arr, r_fwd).wait()
     cos, sin = tw[0], tw[1]
-
-    def forward(k, carry):
-        hi, lo = split(arr[k])
-        y = dot(c1[...], jnp.concatenate([hi, lo, hi], 0))
-        re, im = y[:QROWS], y[QROWS:]
-        zb[k, :, 0:128] = re * cos + im * sin
-        zb[k, :, 128:256] = im * cos - re * sin
-        return carry
-
-    lax.fori_loop(0, PAIRS, forward, 0, unroll=True)
-    hi, lo = split(zb[...].reshape(PAIRS * QROWS, 256))
-    spectrum = dot(jnp.concatenate([hi, lo, hi], 1), b1[...])
-    base = jnp.where(la < 2, 0, POLAR) + half * NDEV
     lane_k, q = iota((QROWS, 128), 1), iota((QROWS, 128), 0)
     k1 = lax.rem(lane_k, 32)
     live = (q <= 32) & (k1 < K1)
+    base = jnp.where(la < 2, 0, POLAR) + half * NDEV
     keep = live & (jnp.abs(q + 64 * (k1 - 14)) < cut[base + me])
-    spectrum = jnp.where(keep[None], spectrum.reshape(PAIRS, QROWS, 128), 0.0)
-    hi, lo = split(spectrum.reshape(PAIRS * QROWS, 128))
-    zb[...] = dot(jnp.concatenate([hi, lo, hi], 1), b2[...]).reshape(PAIRS, QROWS, 256)
-
-    def backward(k, carry):
-        re, im = zb[k, :, 0:128], zb[k, :, 128:256]
-        turned = jnp.concatenate([re * cos - im * sin, re * sin + im * cos], 0)
-        hi, lo = split(turned)
-        res[k] = dot(c2[...], jnp.concatenate([hi, lo, hi], 0))
-        return carry
-
-    lax.fori_loop(0, PAIRS, backward, 0, unroll=True)
-
-    @pl.when(is_polar)
-    def _():
-        pltpu.make_async_copy(res.at[:, me], ret.at[:, 0, me], r_ret).start()
-
-    @pl.when(is_helper)
-    def _():
-        remote(res.at[:, me], ret.at[:, 1, me], s_ret, r_ret, polar_lat, me).start()
-
-    def send_back(k, carry):
-        d = peer(me, k)
-        remote(res.at[:, d], ret.at[:, half, me], s_ret, r_ret, polar_lat, d).start()
-        return carry
-
-    lax.fori_loop(0, NDEV - 1, send_back, 0)
+
+    def filter_part(part):
+        pairs, s, r = pl.ds(part * SIZE, SIZE), s_ret.at[part], r_ret.at[part]
+        pltpu.make_async_copy(arr.at[pairs], arr.at[pairs], r_fwd.at[part]).wait()
+
+        def forward(k, carry):
+            hi, lo = split(arr[part * SIZE + k])
+            y = dot(c1[...], jnp.concatenate([hi, lo, hi], 0))
+            re, im = y[:QROWS], y[QROWS:]
+            zb[k, :, 0:128] = re * cos + im * sin
+            zb[k, :, 128:256] = im * cos - re * sin
+            return carry
+
+        lax.fori_loop(0, SIZE, forward, 0, unroll=True)
+        hi, lo = split(zb[...].reshape(SIZE * QROWS, 256))
+        spectrum = dot(jnp.concatenate([hi, lo, hi], 1), b1[...])
+        spectrum = jnp.where(keep[None], spectrum.reshape(SIZE, QROWS, 128), 0.0)
+        hi, lo = split(spectrum.reshape(SIZE * QROWS, 128))
+        zb[...] = dot(jnp.concatenate([hi, lo, hi], 1), b2[...]).reshape(SIZE, QROWS, 256)
+
+        def backward(k, carry):
+            re, im = zb[k, :, 0:128], zb[k, :, 128:256]
+            turned = jnp.concatenate([re * cos - im * sin, re * sin + im * cos], 0)
+            hi, lo = split(turned)
+            res[part * SIZE + k] = dot(c2[...], jnp.concatenate([hi, lo, hi], 0))
+            return carry
+
+        lax.fori_loop(0, SIZE, backward, 0, unroll=True)
+
+        @pl.when(is_polar)
+        def _():
+            pltpu.make_async_copy(res.at[pairs, me], ret.at[pairs, 0, me], r).start()
+
+        @pl.when(is_helper)
+        def _():
+            remote(res.at[pairs, me], ret.at[pairs, 1, me], s, r, polar_lat, me).start()
+
+        def send_back(k, carry):
+            d = peer(me, k)
+            remote(res.at[pairs, d], ret.at[pairs, half, me], s, r, polar_lat, d).start()
+            return carry
+
+        lax.fori_loop(0, NDEV - 1, send_back, 0)
+
+    for part in range(PARTS):
+        filter_part(part)
 
     pltpu.make_async_copy(rb, rb, r_nest).wait()
     for g in range(3):
@@ -426,25 +442,33 @@
 
     @pl.when(is_polar)
     def _():
-        pltpu.make_async_copy(ret, ret, r_ret).wait()
+        for part in range(PARTS):
+            back = ret.at[pl.ds(part * SIZE, SIZE)]
+            pltpu.make_async_copy(back, back, r_ret.at[part]).wait()
 
     to_east.wait_send()
     to_west.wait_send()
     pl.when(has_south)(to_south.wait_send)
     pl.when(has_north)(to_north.wait_send)
     others = pl.ds(0, NDEV - 1)
-    pltpu.make_async_copy(res.at[:, others], res.at[:, others], s_fwd).wait()
     pltpu.make_async_copy(sb.at[:, :, others], sb.at[:, :, others], s_nest).wait()
-
-    @pl.when(is_polar)
-    def _():
-        for g in range(NZ):
-            relay(g).wait_send()
-        pltpu.make_async_copy(res.at[:, others], res.at[:, others], s_ret).wait()
+    for part in range(PARTS):
+        gone = res.at[pl.ds(part * SIZE, SIZE), others]
+        pltpu.make_async_copy(gone, gone, s_fwd.at[part]).wait()
+
+    @pl.when(is_polar)
+    def _():
+        for part in range(PARTS):
+            for g in range(NZ):
+                relay(part, g).wait_send()
+            gone = res.at[pl.ds(part * SIZE, SIZE), others]
+            pltpu.make_async_copy(gone, gone, s_ret.at[part]).wait()
 
     @pl.when(is_helper)
     def _():
-        pltpu.make_async_copy(res, res, s_ret).wait()
+        for part in range(PARTS):
+            gone = res.at[pl.ds(part * SIZE, SIZE)]
+            pltpu.make_async_copy(gone, gone, s_ret.at[part]).wait()
 
 
 def place_kernel(upd, nest, ret, out, nest_out, rows, sem):
@@ -517,7 +541,7 @@
             pltpu.VMEM((PAIRS, NDEV, 128), F32),
             pltpu.VMEM((PAIRS, NDEV, 128), F32),
             pltpu.VMEM((PAIRS, NDEV, 128), F32),
-            pltpu.VMEM((PAIRS, QROWS, 256), F32),
+            pltpu.VMEM((SIZE, QROWS, 256), F32),
             pltpu.VMEM((COLS, 128), F32),
             pltpu.VMEM((COLS, 128), F32),
             pltpu.VMEM((FIELDS, LEVELS, 1, ROWS), F32),
@@ -529,8 +553,8 @@
             pltpu.VMEM((3, 2, NDEV, 128), F32),
             pltpu.VMEM((3, 128, 128), F32),
             pltpu.VMEM((48, STRIP * 128), BF16),
-            dma((NZ,)), dma((NZ,)),
-            dma, dma, dma, dma, dma, dma,
+            dma((PARTS * NZ,)), dma((PARTS * NZ,)),
+            dma((PARTS,)), dma((PARTS,)), dma((PARTS,)), dma((PARTS,)), dma, dma,
             dma((4,)), dma((4,)),
         ],
         compiler_params=pltpu.CompilerParams(

time: 39.5 us -> 38.8 us (0.982)
  Pallas kernels: 38.8 us -> 38.1 us
    pallas_call x1, Pallas kernels: 37.6 us -> 36.9 us  [local(): pl.pallas_call(step_kernel, name='dynamics_step', out_shape=[jax.ShapeDty...]
where the time goes in v6:
time: 38.8 us; the launch traced here: 38.7 us
  Pallas kernels  38.1 us (98%)
  between operations  0.64 us (2%)
    pallas_call x1, Pallas kernels, local(): pl.pallas_call(step_kernel, name='dynamics_step', out_shape=[jax.ShapeDty...  36.9 us
    pallas_call x1, Pallas kernels, local(): pl.pallas_call(place_kernel, name='place_filtered', out_shape=[jax.ShapeD...  1.14 us

profile of v6, /device:TPU:1, one launch (start us, length us, event | category | flops | bytes accessed | tf_op | source)
XLA Modules:
  0.0 38.7 jit_solution(11124256712118403190)
XLA Ops:
  0.6 36.9 %dynamics_step.1 = (f32[5,4,56,256]{3,2,1,0:T(8,128)S(1)}, f32[1,5,4,2048]{3,2,1,0:T(4,128)S(1)}, f32[10,2,64,128]{3,2,1,0:T(8,128)S(1)}) custom-call(f32[5,4,56,256]{3,2,1,0:T(8,128)} %ms_hbm.1, f32[2,256]{1,0:T(2,128)} %dif_hbm.1, f32[5,4,5]{2,1,0:T(4,128)} %bitcast.3, s32[256]{0:T(256)} %cut_hbm.1, s32[4,64]{1,0:T(4,128)} %bitcast.4, ...), custom_call_target="tpu_custom_call" | custom-call | tf_op jit(solution)/shard_map/dynamics_step/pallas_call | solution.py:527
  37.6 1.1 %place_filtered.1 = (f32[5,4,56,256]{3,2,1,0:T(8,128)}, f32[1,5,4,2048]{3,2,1,0:T(4,128)}) custom-call(f32[5,4,56,256]{3,2,1,0:T(8,128)S(1)} %get-tuple-element.5.upd, f32[1,5,4,2048]{3,2,1,0:T(4,128)S(1)} %get-tuple-element.6.nest, f32[10,2,64,128]{3,2,1,0:T(8,128)S(1)} %get-tuple-element.7.ret), custom_call_target="tpu_custom_call" | custom-call | tf_op jit(solution)/shard_map/place_filtered/pallas_call | solution.py:564

commit v7 on v6

--- a/solution.py
+++ b/solution.py
@@ -166,7 +166,7 @@
             ss[...] = jnp.where(lane_u == u, own[:, ROWS - 1 : ROWS], ss[...])
         return carry
 
-    lax.fori_loop(0, LEVELS, level, 0)
+    lax.fori_loop(0, LEVELS, level, 0, unroll=2)
 
     @pl.when(is_polar)
     def _():
@@ -186,7 +186,7 @@
             pk[k, 1] = turned[NDEV:]
             return carry
 
-        lax.fori_loop(0, PAIRS, pack, 0, unroll=2)
+        lax.fori_loop(0, PAIRS, pack, 0, unroll=5)
 
     pl.semaphore_wait(barrier, NDEV - 1 + jnp.where(is_polar, 1, 2))
 

time: 38.8 us -> 38.6 us (level)
  no operation moved by 1% of the time
where the time goes in v7:
time: 38.6 us
  Pallas kernels  37.9 us (98%)
  between operations  0.64 us (2%)
    pallas_call x1, Pallas kernels, local(): pl.pallas_call(step_kernel, name='dynamics_step', out_shape=[jax.ShapeDty...  36.8 us
    pallas_call x1, Pallas kernels, local(): pl.pallas_call(place_kernel, name='place_filtered', out_shape=[jax.ShapeD...  1.14 us

profile of v7, /device:TPU:1, one launch (start us, length us, event | category | flops | bytes accessed | tf_op | source)
XLA Modules:
  0.0 38.6 jit_solution(13200603577950439373)
XLA Ops:
  0.6 36.8 %dynamics_step.1 = (f32[5,4,56,256]{3,2,1,0:T(8,128)S(1)}, f32[1,5,4,2048]{3,2,1,0:T(4,128)S(1)}, f32[10,2,64,128]{3,2,1,0:T(8,128)S(1)}) custom-call(f32[5,4,56,256]{3,2,1,0:T(8,128)} %ms_hbm.1, f32[2,256]{1,0:T(2,128)} %dif_hbm.1, f32[5,4,5]{2,1,0:T(4,128)} %bitcast.3, s32[256]{0:T(256)} %cut_hbm.1, s32[4,64]{1,0:T(4,128)} %bitcast.4, ...), custom_call_target="tpu_custom_call" | custom-call | tf_op jit(solution)/shard_map/dynamics_step/pallas_call | solution.py:527
  37.4 1.1 %place_filtered.1 = (f32[5,4,56,256]{3,2,1,0:T(8,128)}, f32[1,5,4,2048]{3,2,1,0:T(4,128)}) custom-call(f32[5,4,56,256]{3,2,1,0:T(8,128)S(1)} %get-tuple-element.5.upd, f32[1,5,4,2048]{3,2,1,0:T(4,128)S(1)} %get-tuple-element.6.nest, f32[10,2,64,128]{3,2,1,0:T(8,128)S(1)} %get-tuple-element.7.ret), custom_call_target="tpu_custom_call" | custom-call | tf_op jit(solution)/shard_map/place_filtered/pallas_call | solution.py:564
